TPU v7x, 256 devices: a whole 4x4x8 slice. The times are simulated.
256 devices in a mesh: span: 32 (over y, z), sector: 8 (over x, core).
Axes of the slice: x: 4, y: 4, z: 8, core: 2. Of those that a mesh axis runs over, the one named last changes fastest.
Arguments:
- velocity: float32 [3, 128, 48, 4096], P(None, 'sector', None, 'span'), may hold values from -6 to 6
- current_speed: float32 [16], replicated, may hold values from 0.25 to 1.5
- current_bin: int32 [4096], P('span'), may hold values from 0 to 15
- face_index: int32 [192], P('sector'), may hold values from 0 to 15, as said below
- quad_weight: float32 [192], P('sector'), may hold values from 0.05 to 0.25
- tension: float32 [4096], P('span'), may hold values from 0.25 to 4
- displacement: float32 [2, 4096], P(None, 'span'), may hold values from -12 to 12
- beam_rate: float32 [2, 4096], P(None, 'span'), may hold values from -12 to 12
Outputs:
- fresh_velocity: float32 [3, 128, 48, 4096], P(None, 'sector', None, 'span')
- sectional_force: float32 [2, 4096], P(None, 'span')
- deflection: float32 [2, 4096], P(None, 'span')
Inputs may be any that keep to these rules, and one draw needn't show every extreme that they name: `face_index`: a wall face of the quadrature point's own sector, counted within that sector's 16 faces; in every sector some point lies on the first face and some on the last.
All inputs are finite; a program needn't handle non-finite values.
Results may differ from a plain program's by a relative error of at most 0.0075.
Values sent between devices are 32-bit elements; how exact they have to be, the bound alone decides.
A program may use at most 192 MiB of HBM per device.

v0:
```python
import math

import jax
import jax.numpy as jnp
from jax import lax
from jax.experimental import pallas as pl
from jax.experimental.pallas import tpu as pltpu
from jax.sharding import PartitionSpec as P

MESH = pl.DeviceIdType.MESH
NU_DT = 0.15
ADV_DT = 0.1
WALL_NU = 0.5
BEAM_EI = 0.5
BEAM_MASS = 0.4
LANES = 128


def roll(x, shift, axis=1):
    size = x.shape[axis]
    return pltpu.roll(x, shift % size if isinstance(shift, int) else shift, axis)


def lane_iota(rows):
    return lax.broadcasted_iota(jnp.int32, (rows, LANES), 1)


def row_iota(rows):
    return lax.broadcasted_iota(jnp.int32, (rows, LANES), 0)


def reduce_chain(A, D, F, rho_of, strides):
    A00, A01, A10, A11 = A
    D00, D01, D11 = D
    Fw, Fs = F
    steps = []
    for s in strides:
        inv = 1.0 / (D00 * D11 - D01 * D01)
        I00, I01, I11 = D11 * inv, -D01 * inv, D00 * inv
        P00 = I00 * A00 + I01 * A10
        P01 = I00 * A01 + I01 * A11
        P10 = I01 * A00 + I11 * A10
        P11 = I01 * A01 + I11 * A11
        E11 = A01 * P01 + A11 * P11
        I00m, I01m, I11m = roll(I00, s), roll(I01, s), roll(I11, s)
        al00 = A00 * I00m + A01 * I01m
        al01 = A00 * I01m + A01 * I11m
        al10 = A10 * I00m + A11 * I01m
        al11 = A10 * I01m + A11 * I11m
        ga00, ga01, ga10, ga11 = roll(P00, -s), roll(P10, -s), roll(P01, -s), roll(P11, -s)
        steps.append((al00, al01, al10, al11, ga00, ga01, ga10, ga11))
        P00m, P01m, P10m, P11m = roll(P00, s), roll(P01, s), roll(P10, s), roll(P11, s)
        D11 = D11 - (al10 * A10 + al11 * A11) - roll(E11, -s)
        Fw, Fs = reduce_load(steps[-1], Fw, Fs, s)
        A00, A01, A10, A11 = (
            -(A00 * P00m + A01 * P10m),
            -(A00 * P01m + A01 * P11m),
            -(A10 * P00m + A11 * P10m),
            -(A10 * P01m + A11 * P11m),
        )
        rw, rs = rho_of(Fw, Fs)
        D00 = rw - A00 - roll(A00, -2 * s)
        D01 = rs - A10 - roll(A01, -2 * s)
    inv = 1.0 / (D00 * D11 - D01 * D01)
    last = (D11 * inv, -D01 * inv, D00 * inv)
    return last[0] * Fw + last[1] * Fs, last[1] * Fw + last[2] * Fs, steps, last


def reduce_load(step, Fw, Fs, s):
    al00, al01, al10, al11, ga00, ga01, ga10, ga11 = step
    Fwm, Fsm, Fwp, Fsp = roll(Fw, s), roll(Fs, s), roll(Fw, -s), roll(Fs, -s)
    return (
        Fw - (al00 * Fwm + al01 * Fsm) - (ga00 * Fwp + ga01 * Fsp),
        Fs - (al10 * Fwm + al11 * Fsm) - (ga10 * Fwp + ga11 * Fsp),
    )


def slab_system(t, mass):
    lane = lane_iota(1)
    g = t / 30.0
    gn = roll(g, -1)
    a00, a01, a10, a11 = (
        -12.0 * BEAM_EI - 36.0 * g,
        -6.0 * BEAM_EI - 3.0 * g,
        6.0 * BEAM_EI + 3.0 * g,
        2.0 * BEAM_EI - g,
    )
    n00, n01, n10, n11 = roll(a00, -1), roll(a01, -1), roll(a10, -1), roll(a11, -1)
    d00 = (12.0 * BEAM_EI + 36.0 * g) + (12.0 * BEAM_EI + 36.0 * gn) + mass
    d01 = (-6.0 * BEAM_EI - 3.0 * g) + (6.0 * BEAM_EI + 3.0 * gn)
    d11 = (4.0 * BEAM_EI + 4.0 * g) + (4.0 * BEAM_EI + 4.0 * gn)
    inside = lane < LANES - 1
    rho_w = jnp.where(inside, (d00 - jnp.maximum(-a00, -n00)) - jnp.minimum(-a00, -n00), 0.0)
    rho_s = jnp.where(inside, (d01 + a10) + n01, 0.0)
    first, last, end = lane == 0, lane == LANES - 2, lane == LANES - 1
    zero = jnp.zeros_like(t)
    row = row_iota(8)

    def stack(rows):
        out = jnp.zeros((8, LANES), jnp.float32)
        for index, value in enumerate(rows):
            out = jnp.where(row == index, value, out)
        return out

    Fw = stack(
        [
            rho_w,
            jnp.where(first, -a00, zero),
            jnp.where(first, -a01, zero),
            jnp.where(last, -n00, jnp.where(end, 1.0, zero)),
            jnp.where(last, -n10, zero),
        ]
    )
    Fs = stack(
        [
            rho_s,
            jnp.where(first, -a10, zero),
            jnp.where(first, -a11, zero),
            jnp.where(last, -n01, zero),
            jnp.where(last, -n11, jnp.where(end, 1.0, zero)),
        ]
    )
    coupled = jnp.logical_and(lane > 0, inside)
    A = tuple(jnp.where(coupled, x, 0.0) for x in (a00, a01, a10, a11))
    D = (jnp.where(inside, d00, 1.0), jnp.where(inside, d01, 0.0), jnp.where(inside, d11, 1.0))

    def rho_of(Fw, Fs):
        return Fw[0:1] + Fw[1:2] + Fw[3:4], Fs[0:1] + Fs[1:2] + Fs[3:4]

    Zw, Zs, steps, inverse = reduce_chain(A, D, (Fw, Fs), rho_of, [1 << b for b in range(7)])
    yw, ys = Zw[0:1], Zs[0:1]
    xa1w, xa1s = Zw[2:3], Zs[2:3]
    xb0w, xb0s, xb1w, xb1s = Zw[3:4], Zs[3:4], Zw[4:5], Zs[4:5]
    numbers = [
        (0, xb0w * a00 + xb0s * a10),
        (0, xb0w * a01 + xb0s * a11),
        (0, xb1w * a00 + xb1s * a10),
        (0, xb1w * a01 + xb1s * a11),
        (0, -(a00 * yw + a10 * ys)),
        (0, -(a01 * yw + a11 * ys)),
        (0, (4.0 * BEAM_EI + 4.0 * g) + (a01 * xa1w + a11 * xa1s)),
        (LANES - 2, -(n00 * yw + n01 * ys)),
        (LANES - 2, -(n10 * yw + n11 * ys)),
        (LANES - 2, (4.0 * BEAM_EI + 4.0 * gn) + (n10 * xb1w + n11 * xb1s)),
    ]
    row16 = row_iota(16)
    table = jnp.zeros((16, LANES), jnp.float32)
    for index, (spot, value) in enumerate(numbers):
        table = jnp.where((row16 == index) & (lane == spot), value, table)
    column = jnp.sum(table, axis=1, keepdims=True)
    message = jnp.sum(jnp.where(lane_iota(16) == row16, column, 0.0), axis=0, keepdims=True)
    answers = jnp.zeros((8, LANES), jnp.float32)
    for u in range(4):
        answers = jnp.where(row // 2 == u, Zw[u + 1 : u + 2], answers)
    return message, answers, steps, inverse


def chain_response(numbers, count, place, mass):
    lane = lane_iota(1)
    valid = lane < count
    row = row_iota(8)
    pick = lambda n: jnp.where(valid, numbers[n : n + 1], 0.0)
    a00, a01, a10, a11 = pick(0), pick(1), pick(2), pick(3)
    raw, ras, ka11, rbw, rbs, kb11 = [pick(n) for n in range(4, 10)]
    above = lambda x: jnp.where(lane < count - 1, roll(x, -1), 0.0)
    first = lane == 0
    rw = rbw + above(raw) + mass - jnp.where(first, a00, 0.0)
    rs = rbs + above(ras) - jnp.where(first, a10, 0.0)
    rw = jnp.where(valid, rw, 1.0)
    rs = jnp.where(valid, rs, 0.0)
    d11 = jnp.where(valid, kb11 + above(ka11), 1.0)
    A = tuple(jnp.where(first, 0.0, x) for x in (a00, a01, a10, a11))
    d00 = rw - A[0] - roll(A[0], -1)
    d01 = rs - A[2] - roll(A[1], -1)
    lane8 = lane_iota(8)
    mine = lane8 == place
    before = lane8 == place - 1
    Fw = jnp.where((before & (row == 0)) | (mine & (row == 2)), 1.0, 0.0)
    Fs = jnp.where((before & (row == 1)) | (mine & (row == 3)), 1.0, 0.0)
    Fw = jnp.where(row == 4, rw, Fw)
    Fs = jnp.where(row == 4, rs, Fs)
    strides = []
    while (1 << len(strides)) < count:
        strides.append(1 << len(strides))
    Gw, Gs, _, _ = reduce_chain(
        A, (d00, d01, d11), (Fw, Fs), lambda w, s: (w[4:5], s[4:5]), strides
    )
    Hw, Hs = roll(Gw, 1), roll(Gs, 1)
    blocks = []
    for u in range(4):
        block = jnp.where(row // 2 == 0, Hw[u : u + 1], 0.0)
        block = jnp.where(row // 2 == 1, Hs[u : u + 1], block)
        block = jnp.where(row // 2 == 2, Gw[u : u + 1], block)
        blocks.append(jnp.where(row // 2 == 3, Gs[u : u + 1], block))
    return blocks


def wide_loads(load):
    row = row_iota(8)
    return jnp.where(row % 2 == 0, load[0:1], load[1:2])


def end_loads(answers, load8):
    total = jnp.sum(answers * load8, axis=1, keepdims=True)
    lane = lane_iota(8)
    keep = (lane % 8 == row_iota(8)) & (lane < 32)
    return jnp.sum(jnp.where(keep, total, 0.0), axis=0, keepdims=True)


def ends_solved(response, loads):
    total = jnp.sum(response * loads, axis=0, keepdims=True)
    lane, row = lane_iota(8), row_iota(8)
    keep = (lane // 8 == row // 2) & (lane % 2 == row % 2) & (lane < 32)
    return jnp.sum(jnp.where(keep, total, 0.0), axis=1, keepdims=True)


def inner_deflection(steps, inverse, load8):
    inside = lane_iota(8) < LANES - 1
    Fw, Fs = jnp.where(inside, load8, 0.0), jnp.zeros((8, LANES), jnp.float32)
    for b in range(7):
        Fw, Fs = reduce_load(steps[b], Fw, Fs, 1 << b)
    return inverse[0] * Fw + inverse[1] * Fs


def kernel(
    count,
    ring,
    vel,
    speed,
    cbin,
    face,
    weight,
    tens,
    disp,
    rate,
    out,
    force_out,
    defl_out,
    V,
    U,
    W,
    TR,
    TL,
    near,
    full,
    PG,
    UG,
    FB,
    KB,
    RB,
    coef,
    OV,
    own_sem,
    send_sem,
    theta_sem,
    near_sem,
    full_sem,
    force_sem,
    stiff_sem,
    load_sem,
    out_sem,
):
    cells, rows = vel.shape[1], vel.shape[2]
    tiles = rows // 8
    base = 8
    k = lax.axis_index("span")
    s = lax.axis_index("sector")
    left, right = lax.rem(k + count - 1, count), lax.rem(k + 1, count)
    lower, upper = lax.rem(s + ring - 1, ring), lax.rem(s + 1, ring)
    low_end = jnp.where(k == 0, 1, 0)
    high_end = jnp.where(k == count - 1, 1, 0)
    mass = BEAM_MASS / LANES**2
    stride = cells + 2
    group = 2 * stride

    own_wall = pltpu.make_async_copy(
        vel.at[:, :, pl.ds(0, 8), :],
        V.at[:, pl.ds(2, cells), pl.ds(base, 8), :],
        own_sem.at[0],
    )
    own_bulk = pltpu.make_async_copy(
        vel.at[:, :, pl.ds(8, rows - 8), :],
        V.at[:, pl.ds(2, cells), pl.ds(base + 8, rows - 8), :],
        own_sem.at[1],
    )
    own_wall.start()
    own_bulk.start()

    barrier = pltpu.get_barrier_semaphore()

    def greet(span, sector):
        pl.semaphore_signal(
            barrier, inc=1, device_id={"span": span, "sector": sector}, device_id_type=MESH
        )

    for side in (left, right):
        for turn in (lower, upper):
            greet(side, turn)

    @pl.loop(1, ring)
    def _(d):
        greet(k, lax.rem(s + d, ring))

    @pl.loop(1, count)
    def _(d):
        greet(lax.rem(k + d, count), s)

    lane = lane_iota(1)
    row8 = row_iota(8)
    current = jnp.zeros((1, LANES), jnp.float32)
    for b in range(speed.shape[0]):
        current = current + jnp.where(cbin[...] == b, speed[b], 0.0)
    total_cells = cells * ring

    def angle_of(index):
        whole = lax.rem(s * cells + index + total_cells, total_cells)
        return 2.0 * math.pi * (whole.astype(jnp.float32) + 0.5) / total_cells

    ring_angle = angle_of(row_iota(24) - 1)
    ring_sin, ring_cos = jnp.sin(ring_angle), jnp.cos(ring_angle)
    face_row = row_iota(24) - 1
    face_weight = jnp.zeros((24, LANES), jnp.float32)
    for q in range(weight.shape[0]):
        face_weight = face_weight + jnp.where(face_row == face[q], weight[q], 0.0)
    coef[0] = face_weight * ring_cos
    coef[1] = face_weight * ring_sin
    coef[2] = -current * ring_sin
    coef[3] = current * ring_cos
    lane_cell = lax.rem(lane, group) // 2 - 1
    lane_angle = angle_of(lane_cell)
    lane_sin, lane_cos = jnp.sin(lane_angle), jnp.cos(lane_angle)

    message, answers, steps, inverse = slab_system(tens[...], mass)
    KB[pl.ds(k, 1), 0, :] = message
    wide = lane_iota(rows)
    even = wide % 2 == 0

    own_wall.wait()
    own_bulk.wait()
    cur_high = jnp.sum(jnp.where(lane == LANES - 1, current, 0.0), axis=1, keepdims=True)
    cur_low = jnp.sum(jnp.where(lane == 0, current, 0.0), axis=1, keepdims=True)

    TR[...] = jnp.where(wide == 3 * group + 1, cur_high, 0.0)
    TL[...] = jnp.where(wide == 3 * group + 2, cur_low, 0.0)

    @pl.loop(0, cells)
    def _(i):
        high, low = TR[...], TL[...]
        for c in range(3):
            spot = c * group + 2 * (i + 1)
            turned = roll(V[c, i + 2, pl.ds(base, rows), :], spot + 2)
            high = jnp.where(wide // 2 == spot // 2, turned, high)
            low = jnp.where(wide // 2 == spot // 2 + 1, turned, low)
        TR[...] = high
        TL[...] = low

    TL[...] = roll(TL[...], -2)

    pl.semaphore_wait(barrier, 4 + (ring - 1) + (count - 1))

    def remote(src, dst, sent, arrived, span, sector):
        return pltpu.make_async_remote_copy(
            src_ref=src,
            dst_ref=dst,
            send_sem=sent,
            recv_sem=arrived,
            device_id={"span": span, "sector": sector},
            device_id_type=MESH,
        )

    spread = [
        (TR, 0, right, s),
        (TL, 1, left, s),
        (TR, 2, right, upper),
        (TL, 3, left, upper),
        (TR, 4, right, lower),
        (TL, 5, left, lower),
    ]
    near_copies = [
        remote(
            src.at[pl.ds(0, 8), :], near.at[slot], send_sem.at[slot], near_sem.at[slot], span, sector
        )
        for src, slot, span, sector in spread
    ]
    full_copies = [
        remote(src, full.at[slot], send_sem.at[6 + slot], full_sem.at[slot], span, sector)
        for src, slot, span, sector in spread
    ]
    theta_copies = []
    for part, (start, size) in enumerate(((0, 8), (8, rows - 8))):
        theta_copies.append(
            remote(
                vel.at[:, pl.ds(0, 2), pl.ds(start, size), :],
                V.at[:, pl.ds(cells + 2, 2), pl.ds(base + start, size), :],
                send_sem.at[12 + 2 * part],
                theta_sem.at[2 * part],
                k,
                lower,
            )
        )
        theta_copies.append(
            remote(
                vel.at[:, pl.ds(cells - 2, 2), pl.ds(start, size), :],
                V.at[:, pl.ds(0, 2), pl.ds(base + start, size), :],
                send_sem.at[13 + 2 * part],
                theta_sem.at[1 + 2 * part],
                k,
                upper,
            )
        )
    for copy in near_copies[2:] + near_copies[:2] + theta_copies[:2]:
        copy.start()
    for copy in theta_copies[2:] + full_copies:
        copy.start()

    @pl.loop(1, count)
    def _(d):
        remote(
            KB.at[k], KB.at[k], send_sem.at[16], stiff_sem, lax.rem(k + d, count), s
        ).start()

    def ghosts(boxes, high, low, depth, store):
        here = lane_iota(depth)
        evens = here % 2 == 0
        at_low = here * 0 + low_end == 1
        at_high = here * 0 + high_end == 1
        ahead = lambda x: roll(x, -1)
        behind = lambda x: roll(x, 1)
        centre = jnp.where(
            evens,
            jnp.where(at_low, low, ahead(boxes[0])),
            jnp.where(at_high, high, behind(boxes[1])),
        )
        outer = jnp.where(
            evens, jnp.where(at_low, low, boxes[0]), jnp.where(at_high, high, boxes[1])
        )
        inner = jnp.where(
            evens, jnp.where(at_low, ahead(low), low), jnp.where(at_high, behind(high), high)
        )
        down = roll(jnp.where(evens, ahead(boxes[2]), behind(boxes[3])), -2 * cells)
        up = roll(jnp.where(evens, ahead(boxes[4]), behind(boxes[5])), 2 * cells)
        own_down, own_up = jnp.zeros_like(down), jnp.zeros_like(up)
        for c in range(3):
            spot = c * group
            turned = roll(V[c, 1, pl.ds(base, depth), :], spot + 1)
            own_down = jnp.where(here // 2 == spot // 2, turned, own_down)
            spot = c * group + 2 * (cells + 1)
            turned = roll(V[c, cells + 2, pl.ds(base, depth), :], spot + 1)
            own_up = jnp.where(here // 2 == spot // 2, turned, own_up)
        own = own_down + own_up
        own = jnp.where(evens, ahead(own), behind(own))
        mirrored = jnp.where(evens, low_end, high_end) == 1
        cell = lax.rem(here, group) // 2 - 1
        in_fields = here < 3 * group
        centre = jnp.where(
            in_fields & (cell == -1),
            jnp.where(mirrored, own, down),
            jnp.where(in_fields & (cell == cells), jnp.where(mirrored, own, up), centre),
        )
        return centre, outer, inner

    def ghost_rates(centre, outer, inner, depth, top):
        here = lane_iota(depth)
        evens = here % 2 == 0
        which = here // group
        ups = {n: roll(centre, n * group) for n in (-2, -1, 1, 2)}
        of = lambda d: jnp.where(
            which == d,
            centre,
            jnp.where(
                which == (d + 1) % 3,
                ups[1] if d < 2 else ups[-2],
                ups[2] if d == 0 else ups[-1],
            ),
        )
        c0, c1, c2 = of(0), of(1), of(2)
        tu, td = roll(centre, -2), roll(centre, 2)
        sub = row_iota(depth)
        ru, rd = roll(centre, -1, 0), roll(centre, 1, 0)
        rd = jnp.where(sub == 0, -centre, rd)
        if top is not None:
            ru = jnp.where(sub == depth - 1, top, ru)
        su, sd = jnp.where(evens, inner, outer), jnp.where(evens, outer, inner)
        return combine(centre, c0, c1, c2, tu, td, ru, rd, su, sd)

    def combine(centre, c0, c1, c2, tu, td, ru, rd, su, sd):
        laplace = (tu + td) + (ru + rd) + (su + sd) - 6.0 * centre
        advect = c0 * (tu - td) + c1 * (ru - rd) + c2 * (su - sd)
        return NU_DT * laplace - (0.5 * ADV_DT) * advect

    def beside(centre, edge, at):
        left_end, right_end = lane_iota(8) == 0, lane_iota(8) == LANES - 1
        turned = roll(edge, lax.rem(2 * LANES - 1 - at, LANES))
        up = roll(jnp.where(left_end, turned, centre), -1)
        down = roll(jnp.where(right_end, turned, centre), 1)
        return up, down

    for copy in near_copies + theta_copies[:2]:
        copy.wait_recv()
    high8, low8 = TR[pl.ds(0, 8), :], TL[pl.ds(0, 8), :]
    centre, outer, inner = ghosts([near[n] for n in range(6)], high8, low8, 8, None)
    edge1 = centre
    edge2 = centre + ghost_rates(centre, outer, inner, 8, None)

    def wall_rates(field, lift, i, edge, fields):
        here = [field(c, i) for c in range(3)]
        rates = []
        for c in range(fields):
            centre = here[c]
            su, sd = beside(centre, edge, c * group + 2 * (i + 1))
            ru = roll(centre, -1, 0)
            rd = jnp.where(row8 == 0, -centre, roll(centre, 1, 0))
            rates.append(
                combine(
                    centre, here[0], here[1], here[2], field(c, i + 1), field(c, i - 1), ru, rd, su, sd
                )
            )
        return here, rates

    @pl.loop(0, cells + 2)
    def _(n):
        here, rates = wall_rates(
            lambda c, i: V[c, i + 2, pl.ds(base, 8), :], None, n - 1, edge1, 3
        )
        for c in range(3):
            W[c, n] = here[c] + rates[c]

    def wall_sum(i, sums):
        x, y = sums
        here, rates = wall_rates(lambda c, i: W[c, i + 1], None, i, edge2, 2)
        fresh = [
            0.5 * (V[c, i + 2, pl.ds(base, 8), :] + here[c] + rates[c]) for c in range(2)
        ]
        wc, ws = coef[0, pl.ds(i + 1, 1), :], coef[1, pl.ds(i + 1, 1), :]
        return (
            x + 2.0 * WALL_NU * (fresh[1] * wc - fresh[0] * ws),
            y + 2.0 * WALL_NU * (fresh[1] * ws + fresh[0] * wc),
        )

    zero8 = jnp.zeros((8, LANES), jnp.float32)
    fx, fy = lax.fori_loop(0, cells, wall_sum, (zero8, zero8))
    FB[s] = jnp.concatenate([fx[0:1], fy[0:1]], axis=0)

    @pl.loop(1, ring)
    def _(d):
        remote(FB.at[s], FB.at[s], send_sem.at[17], force_sem, k, lax.rem(s + d, ring)).start()

    for copy in full_copies + theta_copies[2:]:
        copy.wait_recv()
    centre, outer, inner = ghosts([full[n] for n in range(6)], TR[...], TL[...], rows, None)
    PG[...] = centre
    cur_lo = jnp.sum(
        jnp.where(lane == 3 * group, centre[0:1], 0.0), axis=1, keepdims=True
    )
    cur_hi = jnp.sum(
        jnp.where(lane == 3 * group + 1, centre[0:1], 0.0), axis=1, keepdims=True
    )
    cur_side = jnp.where(lane % 2 == 0, cur_lo, cur_hi)
    top = jnp.where(
        lane // group == 0,
        -cur_side * lane_sin,
        jnp.where(lane // group == 1, cur_side * lane_cos, 0.0),
    )
    UG[...] = centre + ghost_rates(centre, outer, inner, rows, top)

    def outer_rows(i):
        return coef[2, pl.ds(i + 1, 1), :], coef[3, pl.ds(i + 1, 1), :], jnp.zeros((1, LANES), jnp.float32)

    @pl.loop(0, cells + 2)
    def _(n):
        for c, value in enumerate(outer_rows(n - 1)):
            V[c, n + 1, pl.ds(base + rows, 1), :] = value
            V[c, n + 1, pl.ds(base - 1, 1), :] = -V[c, n + 1, pl.ds(base, 1), :]

    def bulk_rates(field, edge, i, t):
        start = base + 8 * t
        here = [field(c, i, start) for c in range(3)]
        rates = []
        for c in range(3):
            su, sd = beside(here[c], edge[pl.ds(8 * t, 8), :], c * group + 2 * (i + 1))
            rates.append(
                combine(
                    here[c],
                    here[0],
                    here[1],
                    here[2],
                    field(c, i + 1, start),
                    field(c, i - 1, start),
                    field(c, i, start + 1),
                    field(c, i, start - 1),
                    su,
                    sd,
                )
            )
        return here, rates

    @pl.loop(0, cells + 2)
    def _(n):
        for t in range(tiles):
            here, rates = bulk_rates(
                lambda c, i, start: V[c, i + 2, pl.ds(start, 8), :], PG, n - 1, t
            )
            for c in range(3):
                fresh = here[c] + rates[c]
                U[c, n, pl.ds(base + 8 * t, 8), :] = fresh
                if t == 0:
                    U[c, n, pl.ds(base - 1, 1), :] = -fresh[0:1]
        for c, value in enumerate(outer_rows(n - 1)):
            U[c, n, pl.ds(base + rows, 1), :] = value

    arrivals = ring - 1
    pltpu.make_async_copy(
        FB.at[pl.ds(0, arrivals)], FB.at[pl.ds(0, arrivals)], force_sem
    ).wait()
    force = FB[0]
    for n in range(1, ring):
        force = force + FB[n]
    force_out[...] = force
    load = force * LANES ** (-1.5) + mass * (disp[...] + rate[...])
    load8 = wide_loads(load)
    RB[pl.ds(k, 1), 0, :] = end_loads(answers, load8)

    @pl.loop(1, count)
    def _(d):
        remote(
            RB.at[k], RB.at[k], send_sem.at[18], load_sem, lax.rem(k + d, count), s
        ).start()

    others = count - 1
    pltpu.make_async_copy(KB.at[pl.ds(0, others)], KB.at[pl.ds(0, others)], stiff_sem).wait()
    spare = jnp.zeros((LANES - count, LANES), jnp.float32)
    numbers = jnp.concatenate([KB[:, 0, :], spare], axis=0).T
    blocks = chain_response(numbers, count, k, mass)
    blocks.append(jnp.zeros((LANES - 32, LANES), jnp.float32))
    response = jnp.concatenate(blocks, axis=0).T[0:count]
    rest = inner_deflection(steps, inverse, load8)

    chunks = 4
    each = cells // chunks
    out_copies = []
    for part in range(chunks):

        @pl.loop(part * each, (part + 1) * each)
        def _(i):
            for t in range(tiles):
                here, rates = bulk_rates(
                    lambda c, i, start: U[c, i + 1, pl.ds(start, 8), :], UG, i, t
                )
                for c in range(3):
                    OV[c, i, pl.ds(8 * t, 8), :] = 0.5 * (
                        V[c, i + 2, pl.ds(base + 8 * t, 8), :] + here[c] + rates[c]
                    )

        copy = pltpu.make_async_copy(
            OV.at[:, pl.ds(part * each, each)],
            out.at[:, pl.ds(part * each, each)],
            out_sem.at[part],
        )
        copy.start()
        out_copies.append(copy)

    pltpu.make_async_copy(RB.at[pl.ds(0, others)], RB.at[pl.ds(0, others)], load_sem).wait()
    ends = ends_solved(response, RB[:, 0, :])
    moved = ends * answers
    for direction in range(2):
        mine = jnp.sum(jnp.where(row8 % 2 == direction, moved, 0.0), axis=0, keepdims=True)
        defl_out[pl.ds(direction, 1), :] = rest[direction : direction + 1] + mine

    for copy in near_copies + full_copies + theta_copies:
        copy.wait_send()
    for sent, size, buffer in ((16, others, KB), (17, arrivals, FB), (18, others, RB)):
        pltpu.make_async_copy(
            buffer.at[pl.ds(0, size)], buffer.at[pl.ds(0, size)], send_sem.at[sent]
        ).wait()
    for copy in out_copies:
        copy.wait()


def solution(mesh):
    count, ring = mesh.shape["span"], mesh.shape["sector"]

    def local(velocity, speed, cbin, face, weight, tension, displacement, beam_rate):
        cells, rows, sections = velocity.shape[1:]
        anywhere = pl.BlockSpec(memory_space=pl.ANY)
        vmem = pl.BlockSpec(memory_space=pltpu.VMEM)
        smem = pl.BlockSpec(memory_space=pltpu.SMEM)
        tall = rows + 16
        f32 = jnp.float32
        return pl.pallas_call(
            lambda *refs: kernel(count, ring, *refs),
            out_shape=(
                jax.ShapeDtypeStruct(velocity.shape, f32),
                jax.ShapeDtypeStruct((2, sections), f32),
                jax.ShapeDtypeStruct((2, sections), f32),
            ),
            in_specs=[anywhere, smem, vmem, smem, smem, vmem, vmem, vmem],
            out_specs=(anywhere, vmem, vmem),
            scratch_shapes=[
                pltpu.VMEM((3, cells + 4, tall, LANES), f32),
                pltpu.VMEM((3, cells + 2, tall, LANES), f32),
                pltpu.VMEM((3, cells + 2, 8, LANES), f32),
                pltpu.VMEM((rows, LANES), f32),
                pltpu.VMEM((rows, LANES), f32),
                pltpu.VMEM((6, 8, LANES), f32),
                pltpu.VMEM((6, rows, LANES), f32),
                pltpu.VMEM((rows, LANES), f32),
                pltpu.VMEM((rows, LANES), f32),
                pltpu.VMEM((ring, 2, LANES), f32),
                pltpu.VMEM((count, 1, LANES), f32),
                pltpu.VMEM((count, 1, LANES), f32),
                pltpu.VMEM((4, 24, LANES), f32),
                pltpu.VMEM((3, cells, rows, LANES), f32),
                pltpu.SemaphoreType.DMA((2,)),
                pltpu.SemaphoreType.DMA((19,)),
                pltpu.SemaphoreType.DMA((4,)),
                pltpu.SemaphoreType.DMA((6,)),
                pltpu.SemaphoreType.DMA((6,)),
                pltpu.SemaphoreType.DMA,
                pltpu.SemaphoreType.DMA,
                pltpu.SemaphoreType.DMA,
                pltpu.SemaphoreType.DMA((4,)),
            ],
            compiler_params=pltpu.CompilerParams(
                collective_id=0, has_side_effects=True, vmem_limit_bytes=48 << 20
            ),
            name="riser",
        )(
            velocity,
            speed,
            cbin.reshape(1, sections),
            face,
            weight,
            tension.reshape(1, sections),
            displacement,
            beam_rate,
        )

    return jax.shard_map(
        local,
        mesh=mesh,
        in_specs=(
            P(None, "sector", None, "span"),
            P(),
            P("span"),
            P("sector"),
            P("sector"),
            P("span"),
            P(None, "span"),
            P(None, "span"),
        ),
        out_specs=(P(None, "sector", None, "span"), P(None, "span"), P(None, "span")),
        check_vma=False,
    )
```

profile of v0, /device:TPU:1, one launch (start us, length us, event | category | flops | bytes accessed | tf_op | source)
XLA Modules:
  0.0 39.2 jit_solution(5626658046022453099)
XLA Ops:
  0.6 0.0 copy-start
  0.6 1.3 %copy-done = f32[3,16,48,128]{3,2,1,0:T(8,128)S(1)} copy-done((f32[3,16,48,128]{3,2,1,0:T(8,128)S(1)}, f32[3,16,48,128]{3,2,1,0:T(8,128)}, u32[]{:S(2)}) %copy-start) | copy-done | bytes 1179672
  1.9 0.0 copy-start.1
  1.9 0.7 %copy-done.1 = f32[2,128]{1,0:T(2,128)S(1)} copy-done((f32[2,128]{1,0:T(2,128)S(1)}, f32[2,128]{1,0:T(2,128)}, u32[]{:S(2)}) %copy-start.1) | copy-done | bytes 1048
  2.6 0.0 copy-start.2
  2.6 0.7 %copy-done.2 = f32[2,128]{1,0:T(2,128)S(1)} copy-done((f32[2,128]{1,0:T(2,128)S(1)}, f32[2,128]{1,0:T(2,128)}, u32[]{:S(2)}) %copy-start.2) | copy-done | bytes 1048
  3.3 0.0 copy-start.3
  3.3 0.7 %copy-done.3 = f32[16]{0:T(128)S(1)} copy-done((f32[16]{0:T(128)S(1)}, f32[16]{0:T(128)}, u32[]{:S(2)}) %copy-start.3) | copy-done | bytes 88
  3.9 0.0 copy-start.4
  3.9 0.7 %copy-done.4 = s32[128]{0:T(128)S(1)} copy-done((s32[128]{0:T(128)S(1)}, s32[128]{0:T(128)}, u32[]{:S(2)}) %copy-start.4) | copy-done | bytes 536
  4.6 0.0 copy-start.5
  4.6 0.7 %copy-done.5 = s32[24]{0:T(128)S(1)} copy-done((s32[24]{0:T(128)S(1)}, s32[24]{0:T(128)}, u32[]{:S(2)}) %copy-start.5) | copy-done | bytes 120
  5.2 0.0 copy-start.6
  5.2 0.7 %copy-done.6 = f32[24]{0:T(128)S(1)} copy-done((f32[24]{0:T(128)S(1)}, f32[24]{0:T(128)}, u32[]{:S(2)}) %copy-start.6) | copy-done | bytes 120
  5.9 0.0 copy-start.7
  5.9 0.7 %copy-done.7 = f32[128]{0:T(128)S(1)} copy-done((f32[128]{0:T(128)S(1)}, f32[128]{0:T(128)}, u32[]{:S(2)}) %copy-start.7) | copy-done | bytes 536
  6.5 30.5 %riser.1 = (f32[3,16,48,128]{3,2,1,0:T(8,128)S(1)}, f32[2,128]{1,0:T(2,128)S(1)}, f32[2,128]{1,0:T(2,128)S(1)}) custom-call(f32[3,16,48,128]{3,2,1,0:T(8,128)S(1)} %copy-done, f32[16]{0:T(128)S(1)} %copy-done.3, s32[1,128]{1,0:T(1,128)S(1)} %bitcast.2, s32[24]{0:T(128)S(1)} %copy-done.5, f32[24]{0:T(128)S(1)} %copy-done.6, f32[1,128]{1,0:T(1,128)S(1)} %bitcast.3, ...), custom_call_target="tpu_custom_call" | custom-call | tf_op jit(solution)/shard_map/riser/pallas_call | solution.py:689
  37.1 1.0 %copy.14 = f32[3,16,48,128]{3,2,1,0:T(8,128)} copy(f32[3,16,48,128]{3,2,1,0:T(8,128)S(1)} %get-tuple-element.6) | data formatting | bytes 2359296
  38.1 0.6 %copy.15 = f32[2,128]{1,0:T(2,128)} copy(f32[2,128]{1,0:T(2,128)S(1)} %get-tuple-element.7) | data formatting | bytes 2048
  38.7 0.6 %copy.16 = f32[2,128]{1,0:T(2,128)} copy(f32[2,128]{1,0:T(2,128)S(1)} %get-tuple-element.8) | data formatting | bytes 2048
Async XLA Ops:
  0.6 1.3 %copy-start = (f32[3,16,48,128]{3,2,1,0:T(8,128)S(1)}, f32[3,16,48,128]{3,2,1,0:T(8,128)}, u32[]{:S(2)}) copy-start(f32[3,16,48,128]{3,2,1,0:T(8,128)} %refs_0_.1) | copy-start | bytes 3538948
  1.9 0.7 %copy-start.1 = (f32[2,128]{1,0:T(2,128)S(1)}, f32[2,128]{1,0:T(2,128)}, u32[]{:S(2)}) copy-start(f32[2,128]{1,0:T(2,128)} %refs_6_.1) | copy-start | bytes 3076
  2.6 0.7 %copy-start.2 = (f32[2,128]{1,0:T(2,128)S(1)}, f32[2,128]{1,0:T(2,128)}, u32[]{:S(2)}) copy-start(f32[2,128]{1,0:T(2,128)} %refs_7_.1) | copy-start | bytes 3076
  3.3 0.7 %copy-start.3 = (f32[16]{0:T(128)S(1)}, f32[16]{0:T(128)}, u32[]{:S(2)}) copy-start(f32[16]{0:T(128)} %refs_1_.1) | copy-start | bytes 196
  3.9 0.7 %copy-start.4 = (s32[128]{0:T(128)S(1)}, s32[128]{0:T(128)}, u32[]{:S(2)}) copy-start(s32[128]{0:T(128)} %param.10) | copy-start | bytes 1540
  4.6 0.7 %copy-start.5 = (s32[24]{0:T(128)S(1)}, s32[24]{0:T(128)}, u32[]{:S(2)}) copy-start(s32[24]{0:T(128)} %refs_3_.1) | copy-start | bytes 292
  5.2 0.7 %copy-start.6 = (f32[24]{0:T(128)S(1)}, f32[24]{0:T(128)}, u32[]{:S(2)}) copy-start(f32[24]{0:T(128)} %refs_4_.1) | copy-start | bytes 292
  5.9 0.7 %copy-start.7 = (f32[128]{0:T(128)S(1)}, f32[128]{0:T(128)}, u32[]{:S(2)}) copy-start(f32[128]{0:T(128)} %param.13) | copy-start | bytes 1540
where the time goes:
time: 39.4 us; the launch traced here: 39.2 us
  Pallas kernels  30.5 us (77%)
  local copies, waits for them, and re-layouts  8.03 us (20%)
  between operations  0.66 us (2%)
    pallas_call x1, Pallas kernels, local(): pl.pallas_call(lambda *refs: kernel(count, ring, *refs), out_shape=(jax.S...  30.5 us
    unnamed x19, local copies, waits for them, and re-layouts  8.03 us

commit v1 on v0

--- a/solution.py
+++ b/solution.py
@@ -225,14 +225,14 @@
 def kernel(
     count,
     ring,
-    vel,
-    speed,
-    cbin,
-    face,
-    weight,
-    tens,
-    disp,
-    rate,
+    vel_hbm,
+    speed_hbm,
+    cbin_hbm,
+    face_hbm,
+    weight_hbm,
+    tens_hbm,
+    disp_hbm,
+    rate_hbm,
     out,
     force_out,
     defl_out,
@@ -241,6 +241,8 @@
     W,
     TR,
     TL,
+    TRw,
+    TLw,
     near,
     full,
     PG,
@@ -249,8 +251,15 @@
     KB,
     RB,
     coef,
-    OV,
+    speed,
+    cbin,
+    face,
+    weight,
+    tens,
+    disp,
+    rate,
     own_sem,
+    small_sem,
     send_sem,
     theta_sem,
     near_sem,
@@ -258,21 +267,43 @@
     force_sem,
     stiff_sem,
     load_sem,
-    out_sem,
+    round_sem,
 ):
+    vel = vel_hbm
     cells, rows = vel.shape[1], vel.shape[2]
     tiles = rows // 8
     base = 8
     k = lax.axis_index("span")
     s = lax.axis_index("sector")
     left, right = lax.rem(k + count - 1, count), lax.rem(k + 1, count)
-    lower, upper = lax.rem(s + ring - 1, ring), lax.rem(s + 1, ring)
+    turn = lambda d: lax.rem(s + d + ring, ring)
+    lower, upper = turn(-1), turn(1)
+    ny = 4 if count >= 32 else 2
+    nz = count // ny
+    y, z = k // nz, lax.rem(k, nz)
+
+    def torus(dy, dz):
+        return lax.rem(y + dy + ny, ny) * nz + lax.rem(z + dz + nz, nz)
+
     low_end = jnp.where(k == 0, 1, 0)
     high_end = jnp.where(k == count - 1, 1, 0)
     mass = BEAM_MASS / LANES**2
     stride = cells + 2
     group = 2 * stride
 
+    barrier = pltpu.get_barrier_semaphore()
+
+    def signal(semaphore, span, sector):
+        pl.semaphore_signal(
+            semaphore, inc=1, device_id={"span": span, "sector": sector}, device_id_type=MESH
+        )
+
+    close = [(side, way) for side in (left, right) for way in (lower, upper)]
+    close += [(k, lower), (k, upper), (left, s), (right, s)]
+    close += [(torus(1, 0), s), (torus(-1, 0), s), (torus(0, 1), s), (torus(0, -1), s)]
+    for span, sector in close:
+        signal(barrier, span, sector)
+
     own_wall = pltpu.make_async_copy(
         vel.at[:, :, pl.ds(0, 8), :],
         V.at[:, pl.ds(2, cells), pl.ds(base, 8), :],
@@ -283,33 +314,48 @@
         V.at[:, pl.ds(2, cells), pl.ds(base + 8, rows - 8), :],
         own_sem.at[1],
     )
+    small = [
+        pltpu.make_async_copy(src, dst, small_sem.at[n])
+        for n, (src, dst) in enumerate(
+            (
+                (speed_hbm, speed),
+                (cbin_hbm, cbin),
+                (face_hbm, face),
+                (weight_hbm, weight),
+                (tens_hbm, tens),
+                (disp_hbm, disp),
+                (rate_hbm, rate),
+            )
+        )
+    ]
     own_wall.start()
+    for copy in small:
+        copy.start()
     own_bulk.start()
 
-    barrier = pltpu.get_barrier_semaphore()
-
-    def greet(span, sector):
-        pl.semaphore_signal(
-            barrier, inc=1, device_id={"span": span, "sector": sector}, device_id_type=MESH
-        )
-
-    for side in (left, right):
-        for turn in (lower, upper):
-            greet(side, turn)
-
-    @pl.loop(1, ring)
-    def _(d):
-        greet(k, lax.rem(s + d, ring))
-
-    @pl.loop(1, count)
-    def _(d):
-        greet(lax.rem(k + d, count), s)
+    rounds = []
+    known = 1
+    while known < max(ring // 2, nz // 2):
+        steps_out = []
+        if known < ring // 2:
+            steps_out += [(k, turn(known)), (k, turn(-known))]
+        if known < nz // 2:
+            steps_out += [(torus(0, known), s), (torus(0, -known), s)]
+        rounds.append(steps_out)
+        known *= 2
+    rows_out = [(torus(1, 0), s), (torus(-1, 0), s)]
+    ring_rounds = len(rounds)
+    rounds += [rows_out, rows_out]
+
+    def begin(n):
+        for span, sector in rounds[n]:
+            signal(round_sem.at[n], span, sector)
+
+    def finish(n):
+        pl.semaphore_wait(round_sem.at[n], len(rounds[n]))
 
     lane = lane_iota(1)
     row8 = row_iota(8)
-    current = jnp.zeros((1, LANES), jnp.float32)
-    for b in range(speed.shape[0]):
-        current = current + jnp.where(cbin[...] == b, speed[b], 0.0)
     total_cells = cells * ring
 
     def angle_of(index):
@@ -318,45 +364,27 @@
 
     ring_angle = angle_of(row_iota(24) - 1)
     ring_sin, ring_cos = jnp.sin(ring_angle), jnp.cos(ring_angle)
-    face_row = row_iota(24) - 1
-    face_weight = jnp.zeros((24, LANES), jnp.float32)
-    for q in range(weight.shape[0]):
-        face_weight = face_weight + jnp.where(face_row == face[q], weight[q], 0.0)
-    coef[0] = face_weight * ring_cos
-    coef[1] = face_weight * ring_sin
-    coef[2] = -current * ring_sin
-    coef[3] = current * ring_cos
     lane_cell = lax.rem(lane, group) // 2 - 1
     lane_angle = angle_of(lane_cell)
     lane_sin, lane_cos = jnp.sin(lane_angle), jnp.cos(lane_angle)
 
-    message, answers, steps, inverse = slab_system(tens[...], mass)
-    KB[pl.ds(k, 1), 0, :] = message
-    wide = lane_iota(rows)
-    even = wide % 2 == 0
-
     own_wall.wait()
-    own_bulk.wait()
-    cur_high = jnp.sum(jnp.where(lane == LANES - 1, current, 0.0), axis=1, keepdims=True)
-    cur_low = jnp.sum(jnp.where(lane == 0, current, 0.0), axis=1, keepdims=True)
-
-    TR[...] = jnp.where(wide == 3 * group + 1, cur_high, 0.0)
-    TL[...] = jnp.where(wide == 3 * group + 2, cur_low, 0.0)
-
-    @pl.loop(0, cells)
-    def _(i):
-        high, low = TR[...], TL[...]
-        for c in range(3):
+    lane8 = lane_iota(8)
+    highs, lows = [], []
+    for c in range(3):
+        high = jnp.zeros((8, LANES), jnp.float32)
+        low = high
+        for i in range(cells):
             spot = c * group + 2 * (i + 1)
-            turned = roll(V[c, i + 2, pl.ds(base, rows), :], spot + 2)
-            high = jnp.where(wide // 2 == spot // 2, turned, high)
-            low = jnp.where(wide // 2 == spot // 2 + 1, turned, low)
-        TR[...] = high
-        TL[...] = low
-
-    TL[...] = roll(TL[...], -2)
-
-    pl.semaphore_wait(barrier, 4 + (ring - 1) + (count - 1))
+            turned = roll(V[c, i + 2, pl.ds(base, 8), :], spot + 2)
+            high = jnp.where(lane8 // 2 == spot // 2, turned, high)
+            low = jnp.where(lane8 // 2 == spot // 2 + 1, turned, low)
+        highs.append(high)
+        lows.append(low)
+    high8 = highs[0] + highs[1] + highs[2]
+    low8 = roll(lows[0] + lows[1] + lows[2], -2)
+    TRw[...] = high8
+    TLw[...] = low8
 
     def remote(src, dst, sent, arrived, span, sector):
         return pltpu.make_async_remote_copy(
@@ -369,22 +397,24 @@
         )
 
     spread = [
-        (TR, 0, right, s),
-        (TL, 1, left, s),
-        (TR, 2, right, upper),
-        (TL, 3, left, upper),
-        (TR, 4, right, lower),
-        (TL, 5, left, lower),
+        (0, 0, right, s),
+        (1, 1, left, s),
+        (0, 2, right, upper),
+        (1, 3, left, upper),
+        (0, 4, right, lower),
+        (1, 5, left, lower),
     ]
     near_copies = [
         remote(
-            src.at[pl.ds(0, 8), :], near.at[slot], send_sem.at[slot], near_sem.at[slot], span, sector
-        )
-        for src, slot, span, sector in spread
+            (TRw, TLw)[which], near.at[slot], send_sem.at[slot], near_sem.at[slot], span, sector
+        )
+        for which, slot, span, sector in spread
     ]
     full_copies = [
-        remote(src, full.at[slot], send_sem.at[6 + slot], full_sem.at[slot], span, sector)
-        for src, slot, span, sector in spread
+        remote(
+            (TR, TL)[which], full.at[slot], send_sem.at[6 + slot], full_sem.at[slot], span, sector
+        )
+        for which, slot, span, sector in spread
     ]
     theta_copies = []
     for part, (start, size) in enumerate(((0, 8), (8, rows - 8))):
@@ -408,16 +438,60 @@
                 upper,
             )
         )
+
+    pl.semaphore_wait(barrier, len(close))
     for copy in near_copies[2:] + near_copies[:2] + theta_copies[:2]:
         copy.start()
-    for copy in theta_copies[2:] + full_copies:
+    begin(0)
+    for copy in theta_copies[2:]:
         copy.start()
 
-    @pl.loop(1, count)
-    def _(d):
-        remote(
-            KB.at[k], KB.at[k], send_sem.at[16], stiff_sem, lax.rem(k + d, count), s
-        ).start()
+    for copy in small:
+        copy.wait()
+    current = jnp.zeros((1, LANES), jnp.float32)
+    for b in range(speed.shape[0]):
+        current = current + jnp.where(cbin[...] == b, speed[b], 0.0)
+    face_row = row_iota(24) - 1
+    face_weight = jnp.zeros((24, LANES), jnp.float32)
+    for q in range(weight.shape[0]):
+        face_weight = face_weight + jnp.where(face_row == face[q], weight[q], 0.0)
+    coef[0] = face_weight * ring_cos
+    coef[1] = face_weight * ring_sin
+    coef[2] = -current * ring_sin
+    coef[3] = current * ring_cos
+    cur_high = jnp.sum(jnp.where(lane == LANES - 1, current, 0.0), axis=1, keepdims=True)
+    cur_low = jnp.sum(jnp.where(lane == 0, current, 0.0), axis=1, keepdims=True)
+    wide = lane_iota(rows)
+    TR[...] = jnp.where(wide == 3 * group + 1, cur_high, 0.0)
+    TL[...] = jnp.where(wide == 3 * group + 2, cur_low, 0.0)
+    own_bulk.wait()
+
+    @pl.loop(0, cells)
+    def _(i):
+        high, low = TR[...], TL[...]
+        for c in range(3):
+            spot = c * group + 2 * (i + 1)
+            turned = roll(V[c, i + 2, pl.ds(base, rows), :], spot + 2)
+            high = jnp.where(wide // 2 == spot // 2, turned, high)
+            low = jnp.where(wide // 2 == spot // 2 + 1, turned, low)
+        TR[...] = high
+        TL[...] = low
+
+    TL[...] = roll(TL[...], -2)
+    for copy in full_copies:
+        copy.start()
+    for n in range(ring_rounds):
+        finish(n)
+        begin(n + 1)
+        if n == 0:
+            message, answers, steps, inverse = slab_system(tens[...], mass)
+            KB[pl.ds(k, 1), 0, :] = message
+
+    def everyone(buffer, sent, arrived):
+        far = [(dy, dz) for dy in range(ny) for dz in range(nz) if (dy, dz) != (0, 0)]
+        far.sort(key=lambda d: -(min(d[0], ny - d[0]) + min(d[1], nz - d[1])))
+        for dy, dz in far:
+            remote(buffer.at[k], buffer.at[k], sent, arrived, torus(dy, dz), s).start()
 
     def ghosts(boxes, high, low, depth, store):
         here = lane_iota(depth)
@@ -497,7 +571,6 @@
 
     for copy in near_copies + theta_copies[:2]:
         copy.wait_recv()
-    high8, low8 = TR[pl.ds(0, 8), :], TL[pl.ds(0, 8), :]
     centre, outer, inner = ghosts([near[n] for n in range(6)], high8, low8, 8, None)
     edge1 = centre
     edge2 = centre + ghost_rates(centre, outer, inner, 8, None)
@@ -517,13 +590,20 @@
             )
         return here, rates
 
-    @pl.loop(0, cells + 2)
-    def _(n):
-        here, rates = wall_rates(
-            lambda c, i: V[c, i + 2, pl.ds(base, 8), :], None, n - 1, edge1, 3
-        )
-        for c in range(3):
-            W[c, n] = here[c] + rates[c]
+    @pl.loop(0, (cells + 2) // 6)
+    def _(block):
+        for n in range(6):
+            n = block * 6 + n
+            here, rates = wall_rates(
+                lambda c, i: V[c, i + 2, pl.ds(base, 8), :], None, n - 1, edge1, 3
+            )
+            for c in range(3):
+                W[c, n] = here[c] + rates[c]
+
+    def wall_block(block, sums):
+        for n in range(8):
+            sums = wall_sum(block * 8 + n, sums)
+        return sums
 
     def wall_sum(i, sums):
         x, y = sums
@@ -538,12 +618,15 @@
         )
 
     zero8 = jnp.zeros((8, LANES), jnp.float32)
-    fx, fy = lax.fori_loop(0, cells, wall_sum, (zero8, zero8))
+    fx, fy = lax.fori_loop(0, cells // 8, wall_block, (zero8, zero8))
     FB[s] = jnp.concatenate([fx[0:1], fy[0:1]], axis=0)
 
     @pl.loop(1, ring)
     def _(d):
         remote(FB.at[s], FB.at[s], send_sem.at[17], force_sem, k, lax.rem(s + d, ring)).start()
+
+    finish(ring_rounds)
+    begin(ring_rounds + 1)
 
     for copy in full_copies + theta_copies[2:]:
         copy.wait_recv()
@@ -608,6 +691,9 @@
         for c, value in enumerate(outer_rows(n - 1)):
             U[c, n, pl.ds(base + rows, 1), :] = value
 
+    finish(ring_rounds + 1)
+    everyone(KB, send_sem.at[16], stiff_sem)
+
     arrivals = ring - 1
     pltpu.make_async_copy(
         FB.at[pl.ds(0, arrivals)], FB.at[pl.ds(0, arrivals)], force_sem
@@ -620,11 +706,7 @@
     load8 = wide_loads(load)
     RB[pl.ds(k, 1), 0, :] = end_loads(answers, load8)
 
-    @pl.loop(1, count)
-    def _(d):
-        remote(
-            RB.at[k], RB.at[k], send_sem.at[18], load_sem, lax.rem(k + d, count), s
-        ).start()
+    everyone(RB, send_sem.at[18], load_sem)
 
     others = count - 1
     pltpu.make_async_copy(KB.at[pl.ds(0, others)], KB.at[pl.ds(0, others)], stiff_sem).wait()
@@ -635,29 +717,16 @@
     response = jnp.concatenate(blocks, axis=0).T[0:count]
     rest = inner_deflection(steps, inverse, load8)
 
-    chunks = 4
-    each = cells // chunks
-    out_copies = []
-    for part in range(chunks):
-
-        @pl.loop(part * each, (part + 1) * each)
-        def _(i):
-            for t in range(tiles):
-                here, rates = bulk_rates(
-                    lambda c, i, start: U[c, i + 1, pl.ds(start, 8), :], UG, i, t
+    @pl.loop(0, cells)
+    def _(i):
+        for t in range(tiles):
+            here, rates = bulk_rates(
+                lambda c, i, start: U[c, i + 1, pl.ds(start, 8), :], UG, i, t
+            )
+            for c in range(3):
+                out[c, i, pl.ds(8 * t, 8), :] = 0.5 * (
+                    V[c, i + 2, pl.ds(base + 8 * t, 8), :] + here[c] + rates[c]
                 )
-                for c in range(3):
-                    OV[c, i, pl.ds(8 * t, 8), :] = 0.5 * (
-                        V[c, i + 2, pl.ds(base + 8 * t, 8), :] + here[c] + rates[c]
-                    )
-
-        copy = pltpu.make_async_copy(
-            OV.at[:, pl.ds(part * each, each)],
-            out.at[:, pl.ds(part * each, each)],
-            out_sem.at[part],
-        )
-        copy.start()
-        out_copies.append(copy)
 
     pltpu.make_async_copy(RB.at[pl.ds(0, others)], RB.at[pl.ds(0, others)], load_sem).wait()
     ends = ends_solved(response, RB[:, 0, :])
@@ -672,7 +741,18 @@
         pltpu.make_async_copy(
             buffer.at[pl.ds(0, size)], buffer.at[pl.ds(0, size)], send_sem.at[sent]
         ).wait()
-    for copy in out_copies:
+
+
+def hand_over(fresh, force, defl, fresh_out, force_out, defl_out, sem):
+    copies = [
+        pltpu.make_async_copy(src, dst, sem.at[n])
+        for n, (src, dst) in enumerate(
+            ((fresh, fresh_out), (force, force_out), (defl, defl_out))
+        )
+    ]
+    for copy in copies:
+        copy.start()
+    for copy in copies:
         copy.wait()
 
 
@@ -681,26 +761,28 @@
 
     def local(velocity, speed, cbin, face, weight, tension, displacement, beam_rate):
         cells, rows, sections = velocity.shape[1:]
-        anywhere = pl.BlockSpec(memory_space=pl.ANY)
+        far = pl.BlockSpec(memory_space=pltpu.HBM)
         vmem = pl.BlockSpec(memory_space=pltpu.VMEM)
-        smem = pl.BlockSpec(memory_space=pltpu.SMEM)
         tall = rows + 16
         f32 = jnp.float32
-        return pl.pallas_call(
+        shapes = (
+            jax.ShapeDtypeStruct(velocity.shape, f32),
+            jax.ShapeDtypeStruct((2, sections), f32),
+            jax.ShapeDtypeStruct((2, sections), f32),
+        )
+        results = pl.pallas_call(
             lambda *refs: kernel(count, ring, *refs),
-            out_shape=(
-                jax.ShapeDtypeStruct(velocity.shape, f32),
-                jax.ShapeDtypeStruct((2, sections), f32),
-                jax.ShapeDtypeStruct((2, sections), f32),
-            ),
-            in_specs=[anywhere, smem, vmem, smem, smem, vmem, vmem, vmem],
-            out_specs=(anywhere, vmem, vmem),
+            out_shape=shapes,
+            in_specs=[far] * 8,
+            out_specs=(vmem,) * 3,
             scratch_shapes=[
                 pltpu.VMEM((3, cells + 4, tall, LANES), f32),
                 pltpu.VMEM((3, cells + 2, tall, LANES), f32),
                 pltpu.VMEM((3, cells + 2, 8, LANES), f32),
                 pltpu.VMEM((rows, LANES), f32),
                 pltpu.VMEM((rows, LANES), f32),
+                pltpu.VMEM((8, LANES), f32),
+                pltpu.VMEM((8, LANES), f32),
                 pltpu.VMEM((6, 8, LANES), f32),
                 pltpu.VMEM((6, rows, LANES), f32),
                 pltpu.VMEM((rows, LANES), f32),
@@ -709,8 +791,15 @@
                 pltpu.VMEM((count, 1, LANES), f32),
                 pltpu.VMEM((count, 1, LANES), f32),
                 pltpu.VMEM((4, 24, LANES), f32),
-                pltpu.VMEM((3, cells, rows, LANES), f32),
+                pltpu.SMEM(speed.shape, f32),
+                pltpu.VMEM((1, sections), jnp.int32),
+                pltpu.SMEM(face.shape, jnp.int32),
+                pltpu.SMEM(weight.shape, f32),
+                pltpu.VMEM((1, sections), f32),
+                pltpu.VMEM((2, sections), f32),
+                pltpu.VMEM((2, sections), f32),
                 pltpu.SemaphoreType.DMA((2,)),
+                pltpu.SemaphoreType.DMA((7,)),
                 pltpu.SemaphoreType.DMA((19,)),
                 pltpu.SemaphoreType.DMA((4,)),
                 pltpu.SemaphoreType.DMA((6,)),
@@ -718,22 +807,30 @@
                 pltpu.SemaphoreType.DMA,
                 pltpu.SemaphoreType.DMA,
                 pltpu.SemaphoreType.DMA,
-                pltpu.SemaphoreType.DMA((4,)),
+                pltpu.SemaphoreType.REGULAR((6,)),
             ],
             compiler_params=pltpu.CompilerParams(
-                collective_id=0, has_side_effects=True, vmem_limit_bytes=48 << 20
+                collective_id=0, has_side_effects=True, vmem_limit_bytes=24 << 20
             ),
             name="riser",
         )(
-            velocity,
+            *[pltpu.with_memory_space_constraint(x, pltpu.HBM) for x in (velocity,
             speed,
             cbin.reshape(1, sections),
             face,
             weight,
             tension.reshape(1, sections),
             displacement,
-            beam_rate,
-        )
+            beam_rate)],
+        )
+        return pl.pallas_call(
+            hand_over,
+            out_shape=shapes,
+            in_specs=[vmem] * 3,
+            out_specs=(far,) * 3,
+            scratch_shapes=[pltpu.SemaphoreType.DMA((3,))],
+            name="results",
+        )(*[pltpu.with_memory_space_constraint(x, pltpu.VMEM) for x in results])
 
     return jax.shard_map(
         local,

time: 39.4 us -> 31.6 us (0.80)
  local copies, waits for them, and re-layouts: 8.03 us -> 0 us
  Pallas kernels: 30.5 us -> 30.9 us
    unnamed x19 -> x0, local copies, waits for them, and re-layouts: 8.03 us -> none
    pallas_call x1 -> x2, Pallas kernels: 30.5 us -> 30.9 us  [the longest x1 29.8 us: local(): pl.pallas_call(lambda *refs: kernel(count, ring, *refs), out_shape=shapes...]
where the time goes in v1:
time: 31.6 us; the launch traced here: 31.5 us
  Pallas kernels  30.9 us (98%)
  between operations  0.64 us (2%)
    pallas_call x1, Pallas kernels, local(): pl.pallas_call(lambda *refs: kernel(count, ring, *refs), out_shape=shapes...  29.8 us
    pallas_call x1, Pallas kernels, local(): pl.pallas_call(hand_over, out_shape=shapes, in_specs=[vmem] * 3, out_spec...  1.05 us

profile of v1, /device:TPU:1, one launch (start us, length us, event | category | flops | bytes accessed | tf_op | source)
XLA Modules:
  0.0 31.5 jit_solution(10493315390579999758)
XLA Ops:
  0.6 29.8 %riser.1 = (f32[3,16,48,128]{3,2,1,0:T(8,128)S(1)}, f32[2,128]{1,0:T(2,128)S(1)}, f32[2,128]{1,0:T(2,128)S(1)}) custom-call(f32[3,16,48,128]{3,2,1,0:T(8,128)} %refs_0_.1, f32[16]{0:T(128)} %refs_1_.1, s32[1,128]{1,0:T(1,128)} %bitcast.2, s32[24]{0:T(128)} %refs_3_.1, f32[24]{0:T(128)} %refs_4_.1, f32[1,128]{1,0:T(1,128)} %bitcast.3, f32[2,128]{1,0:T(2,128)} %refs_6_.1, ...), custom_call_target="tpu_custom_call" | custom-call | tf_op jit(solution)/shard_map/riser/pallas_call | solution.py:773
  30.5 1.0 %results.1 = (f32[3,16,48,128]{3,2,1,0:T(8,128)}, f32[2,128]{1,0:T(2,128)}, f32[2,128]{1,0:T(2,128)}) custom-call(f32[3,16,48,128]{3,2,1,0:T(8,128)S(1)} %get-tuple-element.6.fresh, f32[2,128]{1,0:T(2,128)S(1)} %get-tuple-element.7.force, f32[2,128]{1,0:T(2,128)S(1)} %get-tuple-element.8.defl), custom_call_target="tpu_custom_call" | custom-call | tf_op jit(solution)/shard_map/results/pallas_call | solution.py:826

commit v2 on v1

--- a/solution.py
+++ b/solution.py
@@ -301,9 +301,6 @@
     close = [(side, way) for side in (left, right) for way in (lower, upper)]
     close += [(k, lower), (k, upper), (left, s), (right, s)]
     close += [(torus(1, 0), s), (torus(-1, 0), s), (torus(0, 1), s), (torus(0, -1), s)]
-    for span, sector in close:
-        signal(barrier, span, sector)
-
     own_wall = pltpu.make_async_copy(
         vel.at[:, :, pl.ds(0, 8), :],
         V.at[:, pl.ds(2, cells), pl.ds(base, 8), :],
@@ -332,6 +329,9 @@
     for copy in small:
         copy.start()
     own_bulk.start()
+
+    for span, sector in close:
+        signal(barrier, span, sector)
 
     rounds = []
     known = 1
@@ -438,13 +438,6 @@
                 upper,
             )
         )
-
-    pl.semaphore_wait(barrier, len(close))
-    for copy in near_copies[2:] + near_copies[:2] + theta_copies[:2]:
-        copy.start()
-    begin(0)
-    for copy in theta_copies[2:]:
-        copy.start()
 
     for copy in small:
         copy.wait()
@@ -478,14 +471,18 @@
         TL[...] = low
 
     TL[...] = roll(TL[...], -2)
-    for copy in full_copies:
+    pl.semaphore_wait(barrier, len(close))
+    for copy in near_copies[2:] + near_copies[:2] + theta_copies[:2]:
         copy.start()
+    begin(0)
+    for copy in full_copies[2:] + full_copies[:2] + theta_copies[2:]:
+        copy.start()
+
+    message, answers, steps, inverse = slab_system(tens[...], mass)
+    KB[pl.ds(k, 1), 0, :] = message
     for n in range(ring_rounds):
         finish(n)
         begin(n + 1)
-        if n == 0:
-            message, answers, steps, inverse = slab_system(tens[...], mass)
-            KB[pl.ds(k, 1), 0, :] = message
 
     def everyone(buffer, sent, arrived):
         far = [(dy, dz) for dy in range(ny) for dz in range(nz) if (dy, dz) != (0, 0)]
@@ -708,15 +705,6 @@
 
     everyone(RB, send_sem.at[18], load_sem)
 
-    others = count - 1
-    pltpu.make_async_copy(KB.at[pl.ds(0, others)], KB.at[pl.ds(0, others)], stiff_sem).wait()
-    spare = jnp.zeros((LANES - count, LANES), jnp.float32)
-    numbers = jnp.concatenate([KB[:, 0, :], spare], axis=0).T
-    blocks = chain_response(numbers, count, k, mass)
-    blocks.append(jnp.zeros((LANES - 32, LANES), jnp.float32))
-    response = jnp.concatenate(blocks, axis=0).T[0:count]
-    rest = inner_deflection(steps, inverse, load8)
-
     @pl.loop(0, cells)
     def _(i):
         for t in range(tiles):
@@ -727,6 +715,15 @@
                 out[c, i, pl.ds(8 * t, 8), :] = 0.5 * (
                     V[c, i + 2, pl.ds(base + 8 * t, 8), :] + here[c] + rates[c]
                 )
+
+    others = count - 1
+    pltpu.make_async_copy(KB.at[pl.ds(0, others)], KB.at[pl.ds(0, others)], stiff_sem).wait()
+    spare = jnp.zeros((LANES - count, LANES), jnp.float32)
+    numbers = jnp.concatenate([KB[:, 0, :], spare], axis=0).T
+    blocks = chain_response(numbers, count, k, mass)
+    blocks.append(jnp.zeros((LANES - 32, LANES), jnp.float32))
+    response = jnp.concatenate(blocks, axis=0).T[0:count]
+    rest = inner_deflection(steps, inverse, load8)
 
     pltpu.make_async_copy(RB.at[pl.ds(0, others)], RB.at[pl.ds(0, others)], load_sem).wait()
     ends = ends_solved(response, RB[:, 0, :])

time: 31.6 us -> 27.6 us (0.87)
  Pallas kernels: 30.9 us -> 26.9 us
    pallas_call x1, Pallas kernels: 29.8 us -> 25.8 us  [local(): pl.pallas_call(lambda *refs: kernel(count, ring, *refs), out_shape=shapes...]
where the time goes in v2:
time: 27.6 us; the launch traced here: 27.5 us
  Pallas kernels  26.9 us (97%)
  between operations  0.64 us (2%)
    pallas_call x1, Pallas kernels, local(): pl.pallas_call(lambda *refs: kernel(count, ring, *refs), out_shape=shapes...  25.8 us
    pallas_call x1, Pallas kernels, local(): pl.pallas_call(hand_over, out_shape=shapes, in_specs=[vmem] * 3, out_spec...  1.05 us

profile of v2, /device:TPU:1, one launch (start us, length us, event | category | flops | bytes accessed | tf_op | source)
XLA Modules:
  0.0 27.5 jit_solution(8498865017368690145)
XLA Ops:
  0.6 25.8 %riser.1 = (f32[3,16,48,128]{3,2,1,0:T(8,128)S(1)}, f32[2,128]{1,0:T(2,128)S(1)}, f32[2,128]{1,0:T(2,128)S(1)}) custom-call(f32[3,16,48,128]{3,2,1,0:T(8,128)} %refs_0_.1, f32[16]{0:T(128)} %refs_1_.1, s32[1,128]{1,0:T(1,128)} %bitcast.2, s32[24]{0:T(128)} %refs_3_.1, f32[24]{0:T(128)} %refs_4_.1, f32[1,128]{1,0:T(1,128)} %bitcast.3, f32[2,128]{1,0:T(2,128)} %refs_6_.1, ...), custom_call_target="tpu_custom_call" | custom-call | tf_op jit(solution)/shard_map/riser/pallas_call | solution.py:770
  26.4 1.0 %results.1 = (f32[3,16,48,128]{3,2,1,0:T(8,128)}, f32[2,128]{1,0:T(2,128)}, f32[2,128]{1,0:T(2,128)}) custom-call(f32[3,16,48,128]{3,2,1,0:T(8,128)S(1)} %get-tuple-element.6.fresh, f32[2,128]{1,0:T(2,128)S(1)} %get-tuple-element.7.force, f32[2,128]{1,0:T(2,128)S(1)} %get-tuple-element.8.defl), custom_call_target="tpu_custom_call" | custom-call | tf_op jit(solution)/shard_map/results/pallas_call | solution.py:823

commit v3 on v2

--- a/solution.py
+++ b/solution.py
@@ -14,6 +14,7 @@
 BEAM_EI = 0.5
 BEAM_MASS = 0.4
 LANES = 128
+CUTS = (3, 9)
 
 
 def roll(x, shift, axis=1):
@@ -268,6 +269,7 @@
     stiff_sem,
     load_sem,
     round_sem,
+    shifts,
 ):
     vel = vel_hbm
     cells, rows = vel.shape[1], vel.shape[2]
@@ -299,7 +301,7 @@
         )
 
     close = [(side, way) for side in (left, right) for way in (lower, upper)]
-    close += [(k, lower), (k, upper), (left, s), (right, s)]
+    close += [(left, s), (right, s)] + [(k, turn(d)) for d in range(1, ring)]
     close += [(torus(1, 0), s), (torus(-1, 0), s), (torus(0, 1), s), (torus(0, -1), s)]
     own_wall = pltpu.make_async_copy(
         vel.at[:, :, pl.ds(0, 8), :],
@@ -330,22 +332,16 @@
         copy.start()
     own_bulk.start()
 
+
     for span, sector in close:
         signal(barrier, span, sector)
 
     rounds = []
     known = 1
-    while known < max(ring // 2, nz // 2):
-        steps_out = []
-        if known < ring // 2:
-            steps_out += [(k, turn(known)), (k, turn(-known))]
-        if known < nz // 2:
-            steps_out += [(torus(0, known), s), (torus(0, -known), s)]
-        rounds.append(steps_out)
+    while known < nz // 2:
+        rounds.append([(torus(0, known), s), (torus(0, -known), s)])
         known *= 2
-    rows_out = [(torus(1, 0), s), (torus(-1, 0), s)]
-    ring_rounds = len(rounds)
-    rounds += [rows_out, rows_out]
+    rounds += [[(torus(1, 0), s), (torus(-1, 0), s)]] * 2
 
     def begin(n):
         for span, sector in rounds[n]:
@@ -367,6 +363,12 @@
     lane_cell = lax.rem(lane, group) // 2 - 1
     lane_angle = angle_of(lane_cell)
     lane_sin, lane_cos = jnp.sin(lane_angle), jnp.cos(lane_angle)
+
+    from_lane = lax.broadcasted_iota(jnp.int32, (LANES, 2 * LANES), 0)
+    to_lane = lax.broadcasted_iota(jnp.int32, (LANES, 2 * LANES), 1)
+    source = jnp.where(to_lane < LANES, to_lane + 1, to_lane - LANES - 1)
+    source = jnp.where(to_lane == LANES - 1, -1, source)
+    shifts[...] = jnp.where(from_lane == source, 1.0, 0.0).astype(jnp.bfloat16)
 
     own_wall.wait()
     lane8 = lane_iota(8)
@@ -480,9 +482,17 @@
 
     message, answers, steps, inverse = slab_system(tens[...], mass)
     KB[pl.ds(k, 1), 0, :] = message
-    for n in range(ring_rounds):
-        finish(n)
-        begin(n + 1)
+    advance = iter(range(len(rounds)))
+
+    def next_round():
+        n = next(advance, None)
+        if n is not None:
+            finish(n)
+            if n + 1 < len(rounds):
+                begin(n + 1)
+
+    for _ in range(len(rounds) - 2):
+        next_round()
 
     def everyone(buffer, sent, arrived):
         far = [(dy, dz) for dy in range(ny) for dz in range(nz) if (dy, dz) != (0, 0)]
@@ -622,13 +632,13 @@
     def _(d):
         remote(FB.at[s], FB.at[s], send_sem.at[17], force_sem, k, lax.rem(s + d, ring)).start()
 
-    finish(ring_rounds)
-    begin(ring_rounds + 1)
+    next_round()
 
     for copy in full_copies + theta_copies[2:]:
         copy.wait_recv()
     centre, outer, inner = ghosts([full[n] for n in range(6)], TR[...], TL[...], rows, None)
-    PG[...] = centre
+    swap = lambda x: jnp.where(lane_iota(rows) % 2 == 0, roll(x, -1), roll(x, 1))
+    PG[...] = swap(centre)
     cur_lo = jnp.sum(
         jnp.where(lane == 3 * group, centre[0:1], 0.0), axis=1, keepdims=True
     )
@@ -641,7 +651,7 @@
         -cur_side * lane_sin,
         jnp.where(lane // group == 1, cur_side * lane_cos, 0.0),
     )
-    UG[...] = centre + ghost_rates(centre, outer, inner, rows, top)
+    UG[...] = swap(centre + ghost_rates(centre, outer, inner, rows, top))
 
     def outer_rows(i):
         return coef[2, pl.ds(i + 1, 1), :], coef[3, pl.ds(i + 1, 1), :], jnp.zeros((1, LANES), jnp.float32)
@@ -652,44 +662,51 @@
             V[c, n + 1, pl.ds(base + rows, 1), :] = value
             V[c, n + 1, pl.ds(base - 1, 1), :] = -V[c, n + 1, pl.ds(base, 1), :]
 
-    def bulk_rates(field, edge, i, t):
-        start = base + 8 * t
-        here = [field(c, i, start) for c in range(3)]
-        rates = []
-        for c in range(3):
-            su, sd = beside(here[c], edge[pl.ds(8 * t, 8), :], c * group + 2 * (i + 1))
-            rates.append(
-                combine(
-                    here[c],
-                    here[0],
-                    here[1],
-                    here[2],
-                    field(c, i + 1, start),
-                    field(c, i - 1, start),
-                    field(c, i, start + 1),
-                    field(c, i, start - 1),
-                    su,
-                    sd,
-                )
-            )
-        return here, rates
-
-    @pl.loop(0, cells + 2)
-    def _(n):
+    first_lane, last_lane = lane_iota(8) == 0, lane_iota(8) == LANES - 1
+
+    def advanced(field, edge, i, scale, store):
+        here = [[field(c, i, base + 8 * t) for t in range(tiles)] for c in range(3)]
+        column = jnp.concatenate([tile for own in here for tile in own], axis=0)
+        moved = jnp.dot(
+            column.astype(jnp.bfloat16), shifts[...], preferred_element_type=jnp.float32
+        )
         for t in range(tiles):
-            here, rates = bulk_rates(
-                lambda c, i, start: V[c, i + 2, pl.ds(start, 8), :], PG, n - 1, t
-            )
+            start = base + 8 * t
+            weights = []
+            for d in range(3):
+                half = (0.5 * ADV_DT * scale) * here[d][t]
+                weights.append((NU_DT * scale - half, NU_DT * scale + half))
             for c in range(3):
-                fresh = here[c] + rates[c]
+                line = (c * tiles + t) * 8
+                at = c * group + 2 * (i + 1)
+                ghost = roll(edge[pl.ds(8 * t, 8), :], lax.rem(2 * LANES - 1 - at, LANES))
+                su = jnp.where(last_lane, ghost, moved[line : line + 8, :LANES])
+                sd = jnp.where(first_lane, ghost, moved[line : line + 8, LANES:])
+                total = weights[2][0] * su + weights[2][1] * sd
+                total += weights[0][0] * field(c, i + 1, start)
+                total += weights[0][1] * field(c, i - 1, start)
+                total += weights[1][0] * field(c, i, start + 1)
+                total += weights[1][1] * field(c, i, start - 1)
+                store(c, t, total + (scale * (1.0 - 6.0 * NU_DT)) * here[c][t])
+
+    def first_stage(pair):
+        for n in (2 * pair, 2 * pair + 1):
+
+            def store(c, t, fresh, n=n):
                 U[c, n, pl.ds(base + 8 * t, 8), :] = fresh
                 if t == 0:
                     U[c, n, pl.ds(base - 1, 1), :] = -fresh[0:1]
-        for c, value in enumerate(outer_rows(n - 1)):
-            U[c, n, pl.ds(base + rows, 1), :] = value
-
-    finish(ring_rounds + 1)
+
+            advanced(
+                lambda c, i, start: V[c, i + 2, pl.ds(start, 8), :], PG, n - 1, 1.0, store
+            )
+            for c, value in enumerate(outer_rows(n - 1)):
+                U[c, n, pl.ds(base + rows, 1), :] = value
+
+    pl.loop(0, CUTS[0])(first_stage)
+    next_round()
     everyone(KB, send_sem.at[16], stiff_sem)
+    pl.loop(CUTS[0], CUTS[1])(first_stage)
 
     arrivals = ring - 1
     pltpu.make_async_copy(
@@ -705,16 +722,18 @@
 
     everyone(RB, send_sem.at[18], load_sem)
 
-    @pl.loop(0, cells)
-    def _(i):
-        for t in range(tiles):
-            here, rates = bulk_rates(
-                lambda c, i, start: U[c, i + 1, pl.ds(start, 8), :], UG, i, t
-            )
-            for c in range(3):
-                out[c, i, pl.ds(8 * t, 8), :] = 0.5 * (
-                    V[c, i + 2, pl.ds(base + 8 * t, 8), :] + here[c] + rates[c]
+    pl.loop(CUTS[1], cells // 2 + 1)(first_stage)
+
+    @pl.loop(0, cells // 2)
+    def _(pair):
+        for i in (2 * pair, 2 * pair + 1):
+
+            def store(c, t, value, i=i):
+                out[c, i, pl.ds(8 * t, 8), :] = (
+                    0.5 * V[c, i + 2, pl.ds(base + 8 * t, 8), :] + value
                 )
+
+            advanced(lambda c, i, start: U[c, i + 1, pl.ds(start, 8), :], UG, i, 0.5, store)
 
     others = count - 1
     pltpu.make_async_copy(KB.at[pl.ds(0, others)], KB.at[pl.ds(0, others)], stiff_sem).wait()
@@ -805,6 +824,7 @@
                 pltpu.SemaphoreType.DMA,
                 pltpu.SemaphoreType.DMA,
                 pltpu.SemaphoreType.REGULAR((6,)),
+                pltpu.VMEM((LANES, 2 * LANES), jnp.bfloat16),
             ],
             compiler_params=pltpu.CompilerParams(
                 collective_id=0, has_side_effects=True, vmem_limit_bytes=24 << 20

time: 27.6 us -> 26.2 us (0.949)
  Pallas kernels: 26.9 us -> 25.4 us
    pallas_call x1, Pallas kernels: 25.8 us -> 24.4 us  [local(): pl.pallas_call(lambda *refs: kernel(count, ring, *refs), out_shape=shapes...]
where the time goes in v3:
time: 26.2 us; the launch traced here: 26.1 us
  Pallas kernels  25.4 us (97%)
  between operations  0.64 us (2%)
    pallas_call x1, Pallas kernels, local(): pl.pallas_call(lambda *refs: kernel(count, ring, *refs), out_shape=shapes...  24.4 us
    pallas_call x1, Pallas kernels, local(): pl.pallas_call(hand_over, out_shape=shapes, in_specs=[vmem] * 3, out_spec...  1.05 us

profile of v3, /device:TPU:1, one launch (start us, length us, event | category | flops | bytes accessed | tf_op | source)
XLA Modules:
  0.0 26.1 jit_solution(14578416921263547460)
XLA Ops:
  0.6 24.4 %riser.1 = (f32[3,16,48,128]{3,2,1,0:T(8,128)S(1)}, f32[2,128]{1,0:T(2,128)S(1)}, f32[2,128]{1,0:T(2,128)S(1)}) custom-call(f32[3,16,48,128]{3,2,1,0:T(8,128)} %refs_0_.1, f32[16]{0:T(128)} %refs_1_.1, s32[1,128]{1,0:T(1,128)} %bitcast.2, s32[24]{0:T(128)} %refs_3_.1, f32[24]{0:T(128)} %refs_4_.1, f32[1,128]{1,0:T(1,128)} %bitcast.3, f32[2,128]{1,0:T(2,128)} %refs_6_.1, ...), custom_call_target="tpu_custom_call" | custom-call | tf_op jit(solution)/shard_map/riser/pallas_call | solution.py:789
  25.0 1.0 %results.1 = (f32[3,16,48,128]{3,2,1,0:T(8,128)}, f32[2,128]{1,0:T(2,128)}, f32[2,128]{1,0:T(2,128)}) custom-call(f32[3,16,48,128]{3,2,1,0:T(8,128)S(1)} %get-tuple-element.6.fresh, f32[2,128]{1,0:T(2,128)S(1)} %get-tuple-element.7.force, f32[2,128]{1,0:T(2,128)S(1)} %get-tuple-element.8.defl), custom_call_target="tpu_custom_call" | custom-call | tf_op jit(solution)/shard_map/results/pallas_call | solution.py:843

commit v4 on v3

--- a/solution.py
+++ b/solution.py
@@ -14,7 +14,7 @@
 BEAM_EI = 0.5
 BEAM_MASS = 0.4
 LANES = 128
-CUTS = (3, 9)
+CUTS = (6, 9)
 
 
 def roll(x, shift, axis=1):
@@ -269,7 +269,11 @@
     stiff_sem,
     load_sem,
     round_sem,
+    T,
+    wall_next,
     shifts,
+    shift_a,
+    shift_b,
 ):
     vel = vel_hbm
     cells, rows = vel.shape[1], vel.shape[2]
@@ -371,22 +375,21 @@
     shifts[...] = jnp.where(from_lane == source, 1.0, 0.0).astype(jnp.bfloat16)
 
     own_wall.wait()
-    lane8 = lane_iota(8)
-    highs, lows = [], []
+    TRw[...] = jnp.zeros((24, LANES), jnp.float32)
+    TLw[...] = jnp.zeros((24, LANES), jnp.float32)
+    lanes = lane_iota(cells)
+    high = jnp.zeros((cells, LANES), jnp.float32)
+    low = high
     for c in range(3):
-        high = jnp.zeros((8, LANES), jnp.float32)
-        low = high
-        for i in range(cells):
-            spot = c * group + 2 * (i + 1)
-            turned = roll(V[c, i + 2, pl.ds(base, 8), :], spot + 2)
-            high = jnp.where(lane8 // 2 == spot // 2, turned, high)
-            low = jnp.where(lane8 // 2 == spot // 2 + 1, turned, low)
-        highs.append(high)
-        lows.append(low)
-    high8 = highs[0] + highs[1] + highs[2]
-    low8 = roll(lows[0] + lows[1] + lows[2], -2)
-    TRw[...] = high8
-    TLw[...] = low8
+        for j in range(3):
+            own = V[c, pl.ds(2, cells), base + j, :]
+            T[c, j, pl.ds(2, cells), :] = own
+            spot = c * 3 + j
+            turned = roll(own, 2 * spot + 2)
+            high = jnp.where(lanes // 2 == spot, turned, high)
+            low = jnp.where(lanes // 2 == spot + 1, turned, low)
+    TRw[pl.ds(1, cells), :] = high
+    TLw[pl.ds(1, cells), :] = roll(low, -2)
 
     def remote(src, dst, sent, arrived, span, sector):
         return pltpu.make_async_remote_copy(
@@ -461,6 +464,18 @@
     TL[...] = jnp.where(wide == 3 * group + 2, cur_low, 0.0)
     own_bulk.wait()
 
+    def outer_rows(i):
+        return (
+            coef[2, pl.ds(i + 1, 1), :],
+            coef[3, pl.ds(i + 1, 1), :],
+            jnp.zeros((1, LANES), jnp.float32),
+        )
+
+    def ghost_rows(i):
+        for c, value in enumerate(outer_rows(i)):
+            V[c, i + 2, pl.ds(base + rows, 1), :] = value
+            V[c, i + 2, pl.ds(base - 1, 1), :] = -V[c, i + 2, pl.ds(base, 1), :]
+
     @pl.loop(0, cells)
     def _(i):
         high, low = TR[...], TL[...]
@@ -471,6 +486,7 @@
             low = jnp.where(wide // 2 == spot // 2 + 1, turned, low)
         TR[...] = high
         TL[...] = low
+        ghost_rows(i)
 
     TL[...] = roll(TL[...], -2)
     pl.semaphore_wait(barrier, len(close))
@@ -500,7 +516,7 @@
         for dy, dz in far:
             remote(buffer.at[k], buffer.at[k], sent, arrived, torus(dy, dz), s).start()
 
-    def ghosts(boxes, high, low, depth, store):
+    def ghosts(boxes, high, low, depth):
         here = lane_iota(depth)
         evens = here % 2 == 0
         at_low = here * 0 + low_end == 1
@@ -518,6 +534,13 @@
         inner = jnp.where(
             evens, jnp.where(at_low, ahead(low), low), jnp.where(at_high, behind(high), high)
         )
+        return centre, outer, inner
+
+    def with_corners(centre, boxes, depth):
+        here = lane_iota(depth)
+        evens = here % 2 == 0
+        ahead = lambda x: roll(x, -1)
+        behind = lambda x: roll(x, 1)
         down = roll(jnp.where(evens, ahead(boxes[2]), behind(boxes[3])), -2 * cells)
         up = roll(jnp.where(evens, ahead(boxes[4]), behind(boxes[5])), 2 * cells)
         own_down, own_up = jnp.zeros_like(down), jnp.zeros_like(up)
@@ -538,7 +561,7 @@
             jnp.where(mirrored, own, down),
             jnp.where(in_fields & (cell == cells), jnp.where(mirrored, own, up), centre),
         )
-        return centre, outer, inner
+        return centre
 
     def ghost_rates(centre, outer, inner, depth, top):
         here = lane_iota(depth)
@@ -569,74 +592,101 @@
         advect = c0 * (tu - td) + c1 * (ru - rd) + c2 * (su - sd)
         return NU_DT * laplace - (0.5 * ADV_DT) * advect
 
-    def beside(centre, edge, at):
-        left_end, right_end = lane_iota(8) == 0, lane_iota(8) == LANES - 1
-        turned = roll(edge, lax.rem(2 * LANES - 1 - at, LANES))
-        up = roll(jnp.where(left_end, turned, centre), -1)
-        down = roll(jnp.where(right_end, turned, centre), 1)
-        return up, down
-
     for copy in near_copies + theta_copies[:2]:
         copy.wait_recv()
-    centre, outer, inner = ghosts([near[n] for n in range(6)], high8, low8, 8, None)
-    edge1 = centre
-    edge2 = centre + ghost_rates(centre, outer, inner, 8, None)
-
-    def wall_rates(field, lift, i, edge, fields):
-        here = [field(c, i) for c in range(3)]
-        rates = []
-        for c in range(fields):
-            centre = here[c]
-            su, sd = beside(centre, edge, c * group + 2 * (i + 1))
-            ru = roll(centre, -1, 0)
-            rd = jnp.where(row8 == 0, -centre, roll(centre, 1, 0))
-            rates.append(
-                combine(
-                    centre, here[0], here[1], here[2], field(c, i + 1), field(c, i - 1), ru, rd, su, sd
-                )
+    for c in range(3):
+        for j in range(3):
+            T[c, j, pl.ds(0, 2), :] = V[c, pl.ds(0, 2), base + j, :]
+            T[c, j, pl.ds(cells + 2, 2), :] = V[c, pl.ds(cells + 2, 2), base + j, :]
+    wall_edge, outer, inner = ghosts([near[0], near[1]], TRw[...], TLw[...], 24)
+    here, sub = lane_iota(24), row_iota(24)
+    evens = here % 2 == 0
+    own_first, own_last = jnp.zeros((8, LANES), jnp.float32), jnp.zeros((8, LANES), jnp.float32)
+    lane8 = lane_iota(8)
+    for c in range(3):
+        for j in range(3):
+            spot = c * 3 + j
+            keep = lane8 // 2 == spot
+            own_first = jnp.where(keep, roll(T[c, j, pl.ds(1, 8), :], 2 * spot + 1), own_first)
+            own_last = jnp.where(keep, roll(T[c, j, pl.ds(17, 8), :], 2 * spot + 1), own_last)
+    own = jnp.concatenate([own_first, own_first, own_last], axis=0)
+    own = jnp.where(evens, roll(own, -1), roll(own, 1))
+    down = roll(jnp.where(evens, roll(near[2], -1), roll(near[3], 1)), 24 - cells, 0)
+    up = roll(jnp.where(evens, roll(near[4], -1), roll(near[5], 1)), cells, 0)
+    mirrored = jnp.where(evens, low_end, high_end) == 1
+    wall_edge = jnp.where(
+        sub == 0,
+        jnp.where(mirrored, own, down),
+        jnp.where(sub == cells + 1, jnp.where(mirrored, own, up), wall_edge),
+    )
+
+    def wall_beside(centre, edge, spot, depth):
+        turned = roll(edge, -(2 * spot + 1))
+        places = lane_iota(depth)
+        return (
+            roll(jnp.where(places == 0, turned, centre), -1),
+            roll(jnp.where(places == LANES - 1, turned, centre), 1),
+        )
+
+    which = here // 6
+    turns = {n: roll(wall_edge, 6 * n) for n in (-2, -1, 1, 2)}
+    parts = [
+        jnp.where(which == 0, wall_edge, jnp.where(which == 1, turns[1], turns[2])),
+        jnp.where(which == 1, wall_edge, jnp.where(which == 2, turns[1], turns[-1])),
+        jnp.where(which == 2, wall_edge, jnp.where(which == 1, turns[-1], turns[-2])),
+    ]
+    wall_next[...] = wall_edge + combine(
+        wall_edge,
+        *parts,
+        roll(wall_edge, -1, 0),
+        roll(wall_edge, 1, 0),
+        roll(wall_edge, -2),
+        jnp.where(here // 2 % 3 == 0, -wall_edge, roll(wall_edge, 2)),
+        jnp.where(evens, inner, outer),
+        jnp.where(evens, outer, inner),
+    )
+    for j in range(2):
+        cell = [T[c, j, pl.ds(1, 24), :] for c in range(3)]
+        for c in range(3):
+            su, sd = wall_beside(cell[c], wall_edge, c * 3 + j, 24)
+            W[c, j] = cell[c] + combine(
+                cell[c],
+                *cell,
+                T[c, j, pl.ds(2, 24), :],
+                T[c, j, pl.ds(0, 24), :],
+                T[c, j + 1, pl.ds(1, 24), :],
+                T[c, j - 1, pl.ds(1, 24), :] if j > 0 else -cell[c],
+                su,
+                sd,
             )
-        return here, rates
-
-    @pl.loop(0, (cells + 2) // 6)
-    def _(block):
-        for n in range(6):
-            n = block * 6 + n
-            here, rates = wall_rates(
-                lambda c, i: V[c, i + 2, pl.ds(base, 8), :], None, n - 1, edge1, 3
-            )
-            for c in range(3):
-                W[c, n] = here[c] + rates[c]
-
-    def wall_block(block, sums):
-        for n in range(8):
-            sums = wall_sum(block * 8 + n, sums)
-        return sums
-
-    def wall_sum(i, sums):
-        x, y = sums
-        here, rates = wall_rates(lambda c, i: W[c, i + 1], None, i, edge2, 2)
-        fresh = [
-            0.5 * (V[c, i + 2, pl.ds(base, 8), :] + here[c] + rates[c]) for c in range(2)
-        ]
-        wc, ws = coef[0, pl.ds(i + 1, 1), :], coef[1, pl.ds(i + 1, 1), :]
-        return (
-            x + 2.0 * WALL_NU * (fresh[1] * wc - fresh[0] * ws),
-            y + 2.0 * WALL_NU * (fresh[1] * ws + fresh[0] * wc),
-        )
-
-    zero8 = jnp.zeros((8, LANES), jnp.float32)
-    fx, fy = lax.fori_loop(0, cells // 8, wall_block, (zero8, zero8))
-    FB[s] = jnp.concatenate([fx[0:1], fy[0:1]], axis=0)
-
-    @pl.loop(1, ring)
-    def _(d):
-        remote(FB.at[s], FB.at[s], send_sem.at[17], force_sem, k, lax.rem(s + d, ring)).start()
+    cell = [W[c, 0, pl.ds(1, cells), :] for c in range(3)]
+    fresh = []
+    for c in range(2):
+        su, sd = wall_beside(cell[c], wall_next[pl.ds(1, cells), :], c * 3, cells)
+        rates = combine(
+            cell[c],
+            *cell,
+            W[c, 0, pl.ds(2, cells), :],
+            W[c, 0, pl.ds(0, cells), :],
+            W[c, 1, pl.ds(1, cells), :],
+            -cell[c],
+            su,
+            sd,
+        )
+        fresh.append(0.5 * (T[c, 0, pl.ds(2, cells), :] + cell[c] + rates))
+    wc, ws = coef[0, pl.ds(1, cells), :], coef[1, pl.ds(1, cells), :]
+    fx = jnp.sum(2.0 * WALL_NU * (fresh[1] * wc - fresh[0] * ws), axis=0, keepdims=True)
+    fy = jnp.sum(2.0 * WALL_NU * (fresh[1] * ws + fresh[0] * wc), axis=0, keepdims=True)
+    FB[s] = jnp.concatenate([fx, fy], axis=0)
+    for d in sorted(range(1, ring), key=lambda d: -min(d, ring - d)):
+        remote(FB.at[s], FB.at[s], send_sem.at[17], force_sem, k, turn(d)).start()
 
     next_round()
-
     for copy in full_copies + theta_copies[2:]:
         copy.wait_recv()
-    centre, outer, inner = ghosts([full[n] for n in range(6)], TR[...], TL[...], rows, None)
+    boxes = [full[n] for n in range(6)]
+    centre, outer, inner = ghosts(boxes, TR[...], TL[...], rows)
+    centre = with_corners(centre, boxes, rows)
     swap = lambda x: jnp.where(lane_iota(rows) % 2 == 0, roll(x, -1), roll(x, 1))
     PG[...] = swap(centre)
     cur_lo = jnp.sum(
@@ -653,56 +703,56 @@
     )
     UG[...] = swap(centre + ghost_rates(centre, outer, inner, rows, top))
 
-    def outer_rows(i):
-        return coef[2, pl.ds(i + 1, 1), :], coef[3, pl.ds(i + 1, 1), :], jnp.zeros((1, LANES), jnp.float32)
-
-    @pl.loop(0, cells + 2)
-    def _(n):
-        for c, value in enumerate(outer_rows(n - 1)):
-            V[c, n + 1, pl.ds(base + rows, 1), :] = value
-            V[c, n + 1, pl.ds(base - 1, 1), :] = -V[c, n + 1, pl.ds(base, 1), :]
-
+    ghost_rows(-1)
+    ghost_rows(cells)
     first_lane, last_lane = lane_iota(8) == 0, lane_iota(8) == LANES - 1
 
-    def advanced(field, edge, i, scale, store):
-        here = [[field(c, i, base + 8 * t) for t in range(tiles)] for c in range(3)]
-        column = jnp.concatenate([tile for own in here for tile in own], axis=0)
-        moved = jnp.dot(
+    def shift(field, i, moved):
+        column = jnp.concatenate(
+            [field(c, i, base + 8 * t) for c in range(3) for t in range(tiles)], axis=0
+        )
+        moved[...] = jnp.dot(
             column.astype(jnp.bfloat16), shifts[...], preferred_element_type=jnp.float32
         )
+
+    def advanced(field, edge, i, scale, moved, store):
         for t in range(tiles):
             start = base + 8 * t
+            here = [field(c, i, start) for c in range(3)]
             weights = []
             for d in range(3):
-                half = (0.5 * ADV_DT * scale) * here[d][t]
+                half = (0.5 * ADV_DT * scale) * here[d]
                 weights.append((NU_DT * scale - half, NU_DT * scale + half))
             for c in range(3):
-                line = (c * tiles + t) * 8
+                line = pl.ds((c * tiles + t) * 8, 8)
                 at = c * group + 2 * (i + 1)
                 ghost = roll(edge[pl.ds(8 * t, 8), :], lax.rem(2 * LANES - 1 - at, LANES))
-                su = jnp.where(last_lane, ghost, moved[line : line + 8, :LANES])
-                sd = jnp.where(first_lane, ghost, moved[line : line + 8, LANES:])
+                su = jnp.where(last_lane, ghost, moved[line, pl.ds(0, LANES)])
+                sd = jnp.where(first_lane, ghost, moved[line, pl.ds(LANES, LANES)])
                 total = weights[2][0] * su + weights[2][1] * sd
                 total += weights[0][0] * field(c, i + 1, start)
                 total += weights[0][1] * field(c, i - 1, start)
                 total += weights[1][0] * field(c, i, start + 1)
                 total += weights[1][1] * field(c, i, start - 1)
-                store(c, t, total + (scale * (1.0 - 6.0 * NU_DT)) * here[c][t])
+                store(c, t, total + (scale * (1.0 - 6.0 * NU_DT)) * here[c])
+
+    def from_first(c, i, start):
+        return V[c, i + 2, pl.ds(start, 8), :]
 
     def first_stage(pair):
-        for n in (2 * pair, 2 * pair + 1):
+        for n, ready, later in ((2 * pair, shift_a, shift_b), (2 * pair + 1, shift_b, shift_a)):
 
             def store(c, t, fresh, n=n):
                 U[c, n, pl.ds(base + 8 * t, 8), :] = fresh
                 if t == 0:
                     U[c, n, pl.ds(base - 1, 1), :] = -fresh[0:1]
 
-            advanced(
-                lambda c, i, start: V[c, i + 2, pl.ds(start, 8), :], PG, n - 1, 1.0, store
-            )
+            shift(from_first, n, later)
+            advanced(from_first, PG, n - 1, 1.0, ready, store)
             for c, value in enumerate(outer_rows(n - 1)):
                 U[c, n, pl.ds(base + rows, 1), :] = value
 
+    shift(from_first, -1, shift_a)
     pl.loop(0, CUTS[0])(first_stage)
     next_round()
     everyone(KB, send_sem.at[16], stiff_sem)
@@ -724,16 +774,22 @@
 
     pl.loop(CUTS[1], cells // 2 + 1)(first_stage)
 
+    def from_second(c, i, start):
+        return U[c, i + 1, pl.ds(start, 8), :]
+
+    shift(from_second, 0, shift_a)
+
     @pl.loop(0, cells // 2)
     def _(pair):
-        for i in (2 * pair, 2 * pair + 1):
+        for i, ready, later in ((2 * pair, shift_a, shift_b), (2 * pair + 1, shift_b, shift_a)):
 
             def store(c, t, value, i=i):
                 out[c, i, pl.ds(8 * t, 8), :] = (
                     0.5 * V[c, i + 2, pl.ds(base + 8 * t, 8), :] + value
                 )
 
-            advanced(lambda c, i, start: U[c, i + 1, pl.ds(start, 8), :], UG, i, 0.5, store)
+            shift(from_second, i + 1, later)
+            advanced(from_second, UG, i, 0.5, ready, store)
 
     others = count - 1
     pltpu.make_async_copy(KB.at[pl.ds(0, others)], KB.at[pl.ds(0, others)], stiff_sem).wait()
@@ -794,12 +850,12 @@
             scratch_shapes=[
                 pltpu.VMEM((3, cells + 4, tall, LANES), f32),
                 pltpu.VMEM((3, cells + 2, tall, LANES), f32),
-                pltpu.VMEM((3, cells + 2, 8, LANES), f32),
+                pltpu.VMEM((3, 2, 24, LANES), f32),
                 pltpu.VMEM((rows, LANES), f32),
                 pltpu.VMEM((rows, LANES), f32),
-                pltpu.VMEM((8, LANES), f32),
-                pltpu.VMEM((8, LANES), f32),
-                pltpu.VMEM((6, 8, LANES), f32),
+                pltpu.VMEM((24, LANES), f32),
+                pltpu.VMEM((24, LANES), f32),
+                pltpu.VMEM((6, 24, LANES), f32),
                 pltpu.VMEM((6, rows, LANES), f32),
                 pltpu.VMEM((rows, LANES), f32),
                 pltpu.VMEM((rows, LANES), f32),
@@ -824,7 +880,11 @@
                 pltpu.SemaphoreType.DMA,
                 pltpu.SemaphoreType.DMA,
                 pltpu.SemaphoreType.REGULAR((6,)),
+                pltpu.VMEM((3, 3, 32, LANES), f32),
+                pltpu.VMEM((24, LANES), f32),
                 pltpu.VMEM((LANES, 2 * LANES), jnp.bfloat16),
+                pltpu.VMEM((3 * rows, 2 * LANES), f32),
+                pltpu.VMEM((3 * rows, 2 * LANES), f32),
             ],
             compiler_params=pltpu.CompilerParams(
                 collective_id=0, has_side_effects=True, vmem_limit_bytes=24 << 20

time: 26.2 us -> 25.6 us (0.977)
  Pallas kernels: 25.4 us -> 24.8 us
    pallas_call x1, Pallas kernels: 24.4 us -> 23.8 us  [local(): pl.pallas_call(lambda *refs: kernel(count, ring, *refs), out_shape=shapes...]
where the time goes in v4:
time: 25.6 us; the launch traced here: 25.5 us
  Pallas kernels  24.8 us (97%)
  between operations  0.64 us (2%)
    pallas_call x1, Pallas kernels, local(): pl.pallas_call(lambda *refs: kernel(count, ring, *refs), out_shape=shapes...  23.8 us
    pallas_call x1, Pallas kernels, local(): pl.pallas_call(hand_over, out_shape=shapes, in_specs=[vmem] * 3, out_spec...  1.05 us

profile of v4, /device:TPU:1, one launch (start us, length us, event | category | flops | bytes accessed | tf_op | source)
XLA Modules:
  0.0 25.5 jit_solution(12957884518355584701)
XLA Ops:
  0.6 23.8 %riser.1 = (f32[3,16,48,128]{3,2,1,0:T(8,128)S(1)}, f32[2,128]{1,0:T(2,128)S(1)}, f32[2,128]{1,0:T(2,128)S(1)}) custom-call(f32[3,16,48,128]{3,2,1,0:T(8,128)} %refs_0_.1, f32[16]{0:T(128)} %refs_1_.1, s32[1,128]{1,0:T(1,128)} %bitcast.2, s32[24]{0:T(128)} %refs_3_.1, f32[24]{0:T(128)} %refs_4_.1, f32[1,128]{1,0:T(1,128)} %bitcast.3, f32[2,128]{1,0:T(2,128)} %refs_6_.1, ...), custom_call_target="tpu_custom_call" | custom-call | tf_op jit(solution)/shard_map/riser/pallas_call | solution.py:845
  24.4 1.0 %results.1 = (f32[3,16,48,128]{3,2,1,0:T(8,128)}, f32[2,128]{1,0:T(2,128)}, f32[2,128]{1,0:T(2,128)}) custom-call(f32[3,16,48,128]{3,2,1,0:T(8,128)S(1)} %get-tuple-element.6.fresh, f32[2,128]{1,0:T(2,128)S(1)} %get-tuple-element.7.force, f32[2,128]{1,0:T(2,128)S(1)} %get-tuple-element.8.defl), custom_call_target="tpu_custom_call" | custom-call | tf_op jit(solution)/shard_map/results/pallas_call | solution.py:903

commit v5 on v4

--- a/solution.py
+++ b/solution.py
@@ -14,7 +14,7 @@
 BEAM_EI = 0.5
 BEAM_MASS = 0.4
 LANES = 128
-CUTS = (6, 9)
+CUTS = (5, 7)
 
 
 def roll(x, shift, axis=1):
@@ -269,6 +269,7 @@
     stiff_sem,
     load_sem,
     round_sem,
+    corner,
     T,
     wall_next,
     shifts,
@@ -312,6 +313,12 @@
         V.at[:, pl.ds(2, cells), pl.ds(base, 8), :],
         own_sem.at[0],
     )
+    for span, sector in close[:6]:
+        signal(barrier, span, sector)
+    own_wall.start()
+    for span, sector in close[6:]:
+        signal(barrier, span, sector)
+
     own_bulk = pltpu.make_async_copy(
         vel.at[:, :, pl.ds(8, rows - 8), :],
         V.at[:, pl.ds(2, cells), pl.ds(base + 8, rows - 8), :],
@@ -331,14 +338,10 @@
             )
         )
     ]
-    own_wall.start()
     for copy in small:
         copy.start()
     own_bulk.start()
 
-
-    for span, sector in close:
-        signal(barrier, span, sector)
 
     rounds = []
     known = 1
@@ -409,12 +412,12 @@
         (0, 4, right, lower),
         (1, 5, left, lower),
     ]
-    near_copies = [
-        remote(
-            (TRw, TLw)[which], near.at[slot], send_sem.at[slot], near_sem.at[slot], span, sector
-        )
-        for which, slot, span, sector in spread
-    ]
+    near_copies = []
+    for which, slot, span, sector in spread:
+        src, dst = (TRw, TLw)[which], near.at[slot] if slot < 2 else corner.at[slot - 2]
+        if slot >= 2:
+            src = src.at[pl.ds(cells if slot < 4 else 0, 8), :]
+        near_copies.append(remote(src, dst, send_sem.at[slot], near_sem.at[slot], span, sector))
     full_copies = [
         remote(
             (TR, TL)[which], full.at[slot], send_sem.at[6 + slot], full_sem.at[slot], span, sector
@@ -609,16 +612,18 @@
             keep = lane8 // 2 == spot
             own_first = jnp.where(keep, roll(T[c, j, pl.ds(1, 8), :], 2 * spot + 1), own_first)
             own_last = jnp.where(keep, roll(T[c, j, pl.ds(17, 8), :], 2 * spot + 1), own_last)
-    own = jnp.concatenate([own_first, own_first, own_last], axis=0)
-    own = jnp.where(evens, roll(own, -1), roll(own, 1))
-    down = roll(jnp.where(evens, roll(near[2], -1), roll(near[3], 1)), 24 - cells, 0)
-    up = roll(jnp.where(evens, roll(near[4], -1), roll(near[5], 1)), cells, 0)
-    mirrored = jnp.where(evens, low_end, high_end) == 1
-    wall_edge = jnp.where(
-        sub == 0,
-        jnp.where(mirrored, own, down),
-        jnp.where(sub == cells + 1, jnp.where(mirrored, own, up), wall_edge),
-    )
+    even8 = lane8 % 2 == 0
+    mirrored = jnp.where(even8, low_end, high_end) == 1
+    ends = []
+    for own, left_box, right_box in (
+        (own_first, corner[0], corner[1]),
+        (own_last, corner[2], corner[3]),
+    ):
+        own = jnp.where(even8, roll(own, -1), roll(own, 1))
+        sent = jnp.where(even8, roll(left_box, -1), roll(right_box, 1))
+        ends.append(jnp.where(mirrored, own, sent))
+    ends = jnp.concatenate([ends[0], ends[0], ends[1]], axis=0)
+    wall_edge = jnp.where((sub == 0) | (sub == cells + 1), ends, wall_edge)
 
     def wall_beside(centre, edge, spot, depth):
         turned = roll(edge, -(2 * spot + 1))
@@ -855,7 +860,7 @@
                 pltpu.VMEM((rows, LANES), f32),
                 pltpu.VMEM((24, LANES), f32),
                 pltpu.VMEM((24, LANES), f32),
-                pltpu.VMEM((6, 24, LANES), f32),
+                pltpu.VMEM((2, 24, LANES), f32),
                 pltpu.VMEM((6, rows, LANES), f32),
                 pltpu.VMEM((rows, LANES), f32),
                 pltpu.VMEM((rows, LANES), f32),
@@ -880,6 +885,7 @@
                 pltpu.SemaphoreType.DMA,
                 pltpu.SemaphoreType.DMA,
                 pltpu.SemaphoreType.REGULAR((6,)),
+                pltpu.VMEM((4, 8, LANES), f32),
                 pltpu.VMEM((3, 3, 32, LANES), f32),
                 pltpu.VMEM((24, LANES), f32),
                 pltpu.VMEM((LANES, 2 * LANES), jnp.bfloat16),

time: 25.6 us -> 25.5 us (level)
  no operation moved by 1% of the time
where the time goes in v5:
time: 25.5 us; the launch traced here: 25.4 us
  Pallas kernels  24.7 us (97%)
  between operations  0.64 us (3%)
    pallas_call x1, Pallas kernels, local(): pl.pallas_call(lambda *refs: kernel(count, ring, *refs), out_shape=shapes...  23.7 us
    pallas_call x1, Pallas kernels, local(): pl.pallas_call(hand_over, out_shape=shapes, in_specs=[vmem] * 3, out_spec...  1.05 us

profile of v5, /device:TPU:1, one launch (start us, length us, event | category | flops | bytes accessed | tf_op | source)
XLA Modules:
  0.0 25.4 jit_solution(17102414249856218311)
XLA Ops:
  0.6 23.7 %riser.1 = (f32[3,16,48,128]{3,2,1,0:T(8,128)S(1)}, f32[2,128]{1,0:T(2,128)S(1)}, f32[2,128]{1,0:T(2,128)S(1)}) custom-call(f32[3,16,48,128]{3,2,1,0:T(8,128)} %refs_0_.1, f32[16]{0:T(128)} %refs_1_.1, s32[1,128]{1,0:T(1,128)} %bitcast.2, s32[24]{0:T(128)} %refs_3_.1, f32[24]{0:T(128)} %refs_4_.1, f32[1,128]{1,0:T(1,128)} %bitcast.3, f32[2,128]{1,0:T(2,128)} %refs_6_.1, ...), custom_call_target="tpu_custom_call" | custom-call | tf_op jit(solution)/shard_map/riser/pallas_call | solution.py:850
  24.3 1.0 %results.1 = (f32[3,16,48,128]{3,2,1,0:T(8,128)}, f32[2,128]{1,0:T(2,128)}, f32[2,128]{1,0:T(2,128)}) custom-call(f32[3,16,48,128]{3,2,1,0:T(8,128)S(1)} %get-tuple-element.6.fresh, f32[2,128]{1,0:T(2,128)S(1)} %get-tuple-element.7.force, f32[2,128]{1,0:T(2,128)S(1)} %get-tuple-element.8.defl), custom_call_target="tpu_custom_call" | custom-call | tf_op jit(solution)/shard_map/results/pallas_call | solution.py:909

commit v6 on v5

--- a/solution.py
+++ b/solution.py
@@ -14,7 +14,7 @@
 BEAM_EI = 0.5
 BEAM_MASS = 0.4
 LANES = 128
-CUTS = (5, 7)
+CUTS = (2, 7)
 
 
 def roll(x, shift, axis=1):
@@ -307,7 +307,7 @@
 
     close = [(side, way) for side in (left, right) for way in (lower, upper)]
     close += [(left, s), (right, s)] + [(k, turn(d)) for d in range(1, ring)]
-    close += [(torus(1, 0), s), (torus(-1, 0), s), (torus(0, 1), s), (torus(0, -1), s)]
+    close += [(torus(0, 1), s), (torus(0, -1), s)] + [(torus(d, 0), s) for d in range(1, ny)]
     own_wall = pltpu.make_async_copy(
         vel.at[:, :, pl.ds(0, 8), :],
         V.at[:, pl.ds(2, cells), pl.ds(base, 8), :],
@@ -343,12 +343,12 @@
     own_bulk.start()
 
 
-    rounds = []
+    rounds = [[(torus(0, 1), s), (torus(0, -1), s)]]
     known = 1
     while known < nz // 2:
-        rounds.append([(torus(0, known), s), (torus(0, -known), s)])
-        known *= 2
-    rounds += [[(torus(1, 0), s), (torus(-1, 0), s)]] * 2
+        reach = min(known + 1, nz // 2 - known)
+        rounds.append([(torus(0, reach), s), (torus(0, -reach), s)])
+        known += reach
 
     def begin(n):
         for span, sector in rounds[n]:
@@ -510,7 +510,7 @@
             if n + 1 < len(rounds):
                 begin(n + 1)
 
-    for _ in range(len(rounds) - 2):
+    for _ in range(len(rounds) - 1):
         next_round()
 
     def everyone(buffer, sent, arrived):
@@ -686,7 +686,6 @@
     for d in sorted(range(1, ring), key=lambda d: -min(d, ring - d)):
         remote(FB.at[s], FB.at[s], send_sem.at[17], force_sem, k, turn(d)).start()
 
-    next_round()
     for copy in full_copies + theta_copies[2:]:
         copy.wait_recv()
     boxes = [full[n] for n in range(6)]
@@ -805,19 +804,19 @@
     response = jnp.concatenate(blocks, axis=0).T[0:count]
     rest = inner_deflection(steps, inverse, load8)
 
+    for copy in near_copies + full_copies + theta_copies:
+        copy.wait_send()
+    for sent, size, buffer in ((16, others, KB), (17, arrivals, FB), (18, others, RB)):
+        pltpu.make_async_copy(
+            buffer.at[pl.ds(0, size)], buffer.at[pl.ds(0, size)], send_sem.at[sent]
+        ).wait()
+
     pltpu.make_async_copy(RB.at[pl.ds(0, others)], RB.at[pl.ds(0, others)], load_sem).wait()
     ends = ends_solved(response, RB[:, 0, :])
     moved = ends * answers
     for direction in range(2):
         mine = jnp.sum(jnp.where(row8 % 2 == direction, moved, 0.0), axis=0, keepdims=True)
         defl_out[pl.ds(direction, 1), :] = rest[direction : direction + 1] + mine
-
-    for copy in near_copies + full_copies + theta_copies:
-        copy.wait_send()
-    for sent, size, buffer in ((16, others, KB), (17, arrivals, FB), (18, others, RB)):
-        pltpu.make_async_copy(
-            buffer.at[pl.ds(0, size)], buffer.at[pl.ds(0, size)], send_sem.at[sent]
-        ).wait()
 
 
 def hand_over(fresh, force, defl, fresh_out, force_out, defl_out, sem):

time: 25.5 us -> 25.5 us (level)
  no operation moved by 1% of the time
where the time goes in v6:
time: 25.5 us; the launch traced here: 25.4 us
  Pallas kernels  24.7 us (97%)
  between operations  0.64 us (3%)
    pallas_call x1, Pallas kernels, local(): pl.pallas_call(lambda *refs: kernel(count, ring, *refs), out_shape=shapes...  23.7 us
    pallas_call x1, Pallas kernels, local(): pl.pallas_call(hand_over, out_shape=shapes, in_specs=[vmem] * 3, out_spec...  1.05 us

profile of v6, /device:TPU:1, one launch (start us, length us, event | category | flops | bytes accessed | tf_op | source)
XLA Modules:
  0.0 25.4 jit_solution(15343491860774403309)
XLA Ops:
  0.6 23.7 %riser.1 = (f32[3,16,48,128]{3,2,1,0:T(8,128)S(1)}, f32[2,128]{1,0:T(2,128)S(1)}, f32[2,128]{1,0:T(2,128)S(1)}) custom-call(f32[3,16,48,128]{3,2,1,0:T(8,128)} %refs_0_.1, f32[16]{0:T(128)} %refs_1_.1, s32[1,128]{1,0:T(1,128)} %bitcast.2, s32[24]{0:T(128)} %refs_3_.1, f32[24]{0:T(128)} %refs_4_.1, f32[1,128]{1,0:T(1,128)} %bitcast.3, f32[2,128]{1,0:T(2,128)} %refs_6_.1, ...), custom_call_target="tpu_custom_call" | custom-call | tf_op jit(solution)/shard_map/riser/pallas_call | solution.py:849
  24.3 1.0 %results.1 = (f32[3,16,48,128]{3,2,1,0:T(8,128)}, f32[2,128]{1,0:T(2,128)}, f32[2,128]{1,0:T(2,128)}) custom-call(f32[3,16,48,128]{3,2,1,0:T(8,128)S(1)} %get-tuple-element.6.fresh, f32[2,128]{1,0:T(2,128)S(1)} %get-tuple-element.7.force, f32[2,128]{1,0:T(2,128)S(1)} %get-tuple-element.8.defl), custom_call_target="tpu_custom_call" | custom-call | tf_op jit(solution)/shard_map/results/pallas_call | solution.py:908
